TPU v7x, 768 devices: a whole 4x8x12 slice. The times are simulated.
768 devices in a mesh: seq: 12 (over z_hi, x), head: 64 (over z_lo, y, core).
Axes of the slice: x: 4, y: 8, z: 12 (z_hi: 3, z_lo: 4; z = z_hi * 4 + z_lo), core: 2. Of those that a mesh axis runs over, the one named last changes fastest.
Arguments:
- query_rows: bfloat16 [24576, 64, 128], P('seq', 'head'), may hold values from -112 to 112
- key_rows: bfloat16 [24576, 64, 128], P('seq', 'head'), may hold values from -4 to 4
- value_rows: bfloat16 [24576, 64, 128], P('seq', 'head'), may hold values from -6 to 6
- attn_output: bfloat16 [24576, 64, 128], P('seq', 'head'), may hold values from -6 to 6
- out_grad: bfloat16 [24576, 4, 2048], P(('seq', 'head')), may hold values from -6 to 6
- neighbours: int32 [192, 4], replicated, may hold values from 0 to 191, as said below
- counts: int32 [192], replicated, may hold values from 2 to 128
Outputs:
- grad_query: bfloat16 [24576, 4, 2048], P(('seq', 'head'))
- grad_key: bfloat16 [24576, 4, 2048], P(('seq', 'head'))
- grad_value: bfloat16 [24576, 4, 2048], P(('seq', 'head'))
Inputs may be any that keep to these rules, and one draw needn't show every extreme that they name: `neighbours`: row t lists 4 different tiles, the first being t itself, each at most half of 16 tiles away from t.
All inputs are finite; a program needn't handle non-finite values.
Results may differ from a plain program's by a relative error of at most 0.011.
Values may be sent and summed in bfloat16 or wider, within the bound.
No kernel may reach another device: no remote copies, remote signals or barrier semaphores. Data moves between devices by JAX's collectives and lax.ppermute only.
A program may use at most 64 MiB of HBM per device.

v0:
```python
import jax
import jax.numpy as jnp
from jax import lax
from jax.sharding import PartitionSpec as P

TILE = 128


def with_halo(block, sides, width):
    for axis, dim in sides:
        count = lax.axis_size(axis)
        forward = [(i, i + 1) for i in range(count - 1)]
        backward = [(target, source) for source, target in forward]
        low = lax.ppermute(
            lax.slice_in_dim(block, block.shape[dim] - width, None, axis=dim), axis, forward
        )
        high = lax.ppermute(lax.slice_in_dim(block, 0, width, axis=dim), axis, backward)
        block = jnp.concatenate([low, block, high], axis=dim)
    return block


def pair_block(query, grad_rows, delta_rows, lists, kv_tiles, key_valid, scale_factor, log_rows):
    head_dim = query.shape[-1]
    gathered = kv_tiles[lists]
    key_near = gathered[..., :head_dim]
    value_near = gathered[..., head_dim:]
    valid_near = key_valid[lists]
    scores = (
        jnp.einsum("icgd,injgd->icgnj", query, key_near, preferred_element_type=jnp.float32)
        * scale_factor
    )
    scores = jnp.where(valid_near[:, None, None, :, :], scores, -jnp.inf)
    row_max = jnp.max(scores, axis=(3, 4))
    log_rows = row_max + jnp.log(jnp.sum(jnp.exp(scores - row_max[..., None, None]), axis=(3, 4)))
    attn_probs = jnp.exp(scores - log_rows[..., None, None])
    dprobs = jnp.einsum(
        "icgd,injgd->icgnj", grad_rows, value_near, preferred_element_type=jnp.float32
    )
    dscore = (attn_probs * (dprobs - delta_rows[..., None, None]) * scale_factor).astype(
        jnp.bfloat16
    )
    probs_low = attn_probs.astype(jnp.bfloat16)
    dquery = jnp.einsum("icgnj,injgd->icgd", dscore, key_near, preferred_element_type=jnp.float32)
    dkey_terms = jnp.einsum("icgnj,icgd->injgd", dscore, query, preferred_element_type=jnp.float32)
    dvalue_terms = jnp.einsum(
        "icgnj,icgd->injgd", probs_low, grad_rows, preferred_element_type=jnp.float32
    )
    return (dquery, log_rows, jnp.concatenate([dkey_terms, dvalue_terms], axis=-1))


def per_device(query_rows, key_rows, value_rows, attn_output, out_grad, neighbours, counts):
    seq_rows, batch, width = out_grad.shape
    shard_tokens, group, head_dim = query_rows.shape
    tile_len = TILE
    nbr_count = neighbours.shape[1]
    tiles_all = counts.shape[0]
    tiles_dev = shard_tokens // tile_len
    half_tiles = tiles_dev // 2
    half_tokens = shard_tokens // 2
    scale_factor = head_dim ** (-0.5)
    block_tiles = min(4, tiles_dev)
    block_count = tiles_dev // block_tiles
    grads_in = lax.all_to_all(
        out_grad.reshape(seq_rows, batch * width // head_dim, head_dim),
        "head",
        split_axis=1,
        concat_axis=0,
        tiled=True,
    )
    shard_index = lax.axis_index("seq")
    first_tile = shard_index * tiles_dev
    ext_base = first_tile - half_tiles
    ext_tiles = ext_base + jnp.arange(2 * tiles_dev, dtype=jnp.int32)
    tile_table = jnp.arange(tiles_all, dtype=jnp.int32)
    ext_counts = jnp.sum(
        jnp.where(ext_tiles[:, None] == tile_table[None, :], counts[None, :], 0), axis=1
    )
    positions = jnp.arange(tile_len, dtype=jnp.int32)
    key_valid = positions[None, :] < ext_counts[:, None]
    own_counts = lax.dynamic_slice_in_dim(counts, first_tile, tiles_dev, 0)
    own_valid = (positions[None, :] < own_counts[:, None]).reshape(shard_tokens)
    grad_rows = grads_in * own_valid[:, None, None].astype(jnp.bfloat16)
    delta = jnp.einsum("tgd,tgd->tg", grad_rows, attn_output, preferred_element_type=jnp.float32)
    kv_pairs = jnp.concatenate([key_rows, value_rows], axis=2)
    kv_ext = with_halo(kv_pairs, (("seq", 0),), half_tokens)
    kv_tiles = kv_ext.reshape(2 * tiles_dev, tile_len, group, 2 * head_dim)
    own_lists = lax.dynamic_slice_in_dim(neighbours, first_tile, tiles_dev, 0) - ext_base

    def own_step(totals, inputs):
        query_blk, grad_blk, delta_blk, list_blk = inputs
        dquery, log_blk, dkv_terms = pair_block(
            query_blk, grad_blk, delta_blk, list_blk, kv_tiles, key_valid, scale_factor, None
        )
        totals = totals.at[list_blk.reshape(-1)].add(
            dkv_terms.reshape(-1, tile_len, group, 2 * head_dim)
        )
        return (totals, (dquery, log_blk))

    inputs_own = (
        query_rows.reshape(block_count, block_tiles, tile_len, group, head_dim),
        grad_rows.reshape(block_count, block_tiles, tile_len, group, head_dim),
        delta.reshape(block_count, block_tiles, tile_len, group),
        own_lists.reshape(block_count, block_tiles, nbr_count),
    )
    start_totals = jnp.zeros((2 * tiles_dev, tile_len, group, 2 * head_dim), jnp.float32)
    totals, (dquery_all, log_all) = lax.scan(own_step, start_totals, inputs_own)
    grad_q = dquery_all.reshape(shard_tokens, group, head_dim).astype(jnp.bfloat16)
    totals = totals.reshape(2 * shard_tokens, group, 2 * head_dim)
    middle = totals[half_tokens : half_tokens + shard_tokens]
    flanks = jnp.concatenate([totals[:half_tokens], totals[half_tokens + shard_tokens :]], axis=0)
    returned = with_halo(flanks.astype(jnp.bfloat16), (("seq", 0),), half_tokens).astype(
        flanks.dtype
    )
    own_grads = middle + jnp.concatenate(
        [returned[:half_tokens], returned[half_tokens + shard_tokens :]], axis=0
    )
    grad_k = own_grads[..., :head_dim].astype(jnp.bfloat16)
    grad_v = own_grads[..., head_dim:].astype(jnp.bfloat16)
    back_q, back_k, back_v = (
        lax.all_to_all(grad_q, "head", split_axis=0, concat_axis=1, tiled=True),
        lax.all_to_all(grad_k, "head", split_axis=0, concat_axis=1, tiled=True),
        lax.all_to_all(grad_v, "head", split_axis=0, concat_axis=1, tiled=True),
    )
    return (
        back_q.reshape(seq_rows, batch, width),
        back_k.reshape(seq_rows, batch, width),
        back_v.reshape(seq_rows, batch, width),
    )


def solution(mesh):
    placed = (
        P("seq", "head", None),
        P("seq", "head", None),
        P("seq", "head", None),
        P("seq", "head", None),
        P(("seq", "head"), None, None),
        P(),
        P(),
    )
    return jax.shard_map(
        per_device,
        mesh=mesh,
        in_specs=placed,
        out_specs=(
            P(("seq", "head"), None, None),
            P(("seq", "head"), None, None),
            P(("seq", "head"), None, None),
        ),
        check_vma=False,
    )
```

profile of v0, /device:TPU:263, one launch (start us, length us, event | category | flops | bytes accessed | tf_op | source)
XLA Modules:
  0.0 250.6 jit_solution(6721536808479436578)
XLA Ops:
  3.3 13.5 %all-to-all-start = ((bf16[32,64,128]{2,0,1:T(8,128)(2,1)}), bf16[32,64,128]{2,0,1:T(8,128)(2,1)S(1)}, u32[]{:S(2)}, u32[]{:S(2)}) async-start(bf16[32,64,128]{2,0,1:T(8,128)(2,1)} %copy.79), calls=%async_computation | async-start | bytes 1048576 | tf_op jit(solution)/shard_map/all_to_all | solution.py:63
  17.1 5.7 %collective-permute-start = (bf16[1024,1,256]{2,0,1:T(8,128)(2,1)S(1)}, bf16[1024,1,256]{2,0,1:T(8,128)(2,1)}, u32[]{:S(2)}, u32[]{:S(2)}) collective-permute-start(bf16[1024,1,256]{2,0,1:T(8,128)(2,1)S(1)} %get-tuple-element.156), channel_id=1, source_target_pairs={{0,64},{64,128},{128,192},{192,256},{256,320},{320,384},{384,448},... | collective-permute-start | bytes 1572872 | tf_op jit(solution)/shard_map/ppermute | solution.py:14
  25.5 10.7 %collective-permute-done = bf16[1024,1,256]{2,0,1:T(8,128)(2,1)} collective-permute-done((bf16[1024,1,256]{2,0,1:T(8,128)(2,1)S(1)}, bf16[1024,1,256]{2,0,1:T(8,128)(2,1)}, u32[]{:S(2)}, u32[]{:S(2)}) %collective-permute-start) | collective-permute-done | bytes 524320 | tf_op jit(solution)/shard_map/ppermute | solution.py:14
  36.2 41.2 %collective-permute-done.1 = bf16[1024,1,256]{2,0,1:T(8,128)(2,1)} collective-permute-done((bf16[1024,1,256]{2,0,1:T(8,128)(2,1)S(1)}, bf16[1024,1,256]{2,0,1:T(8,128)(2,1)}, u32[]{:S(2)}, u32[]{:S(2)}) %collective-permute-start.1) | collective-permute-done | bytes 524320 | tf_op jit(solution)/shard_map/ppermute | solution.py:17
  77.4 2.7 %pad_maximum_fusion.1 = bf16[4096,1,256]{2,0,1:T(8,128)(2,1)} fusion(bf16[1024,1,256]{2,0,1:T(8,128)(2,1)} %collective-permute-done.1, bf16[2048,1,256]{2,0,1:T(8,128)(2,1)S(1)} %constant_dynamic-update-slice_fusion.1, bf16[1024,1,256]{2,0,1:T(8,128)(2,1)} %collective-permute-done), kind=kLoop, calls=%fused_computation.47 | loop fusion | flops 6291456 | bytes 4194304 | tf_op jit(solution)/shard_map/concatenate | solution.py:18
  81.1 2.4 broadcast_in_dim.31
  83.5 57.3 %while.13 = (s32[]{:T(128)}, f32[32,128,1,256]{3,1,0,2:T(8,128)}, bf16[4,4,128,1,128]{4,2,1,0,3:T(8,128)(2,1)}, s32[4,4,4]{2,1,0:T(4,128)S(1)}, bf16[4,4,128,1,1...) while((s32[]{:T(128)}, f32[32,128,1,256]{3,1,0,2:T(8,128)}, ...), condition=%wide.region_5.6_spmd.clone, body=%wide.region_1.5_spmd.clone.sunk | while | flops 339743328 | bytes 27432008 | solution.py:106
  84.3 2.2 gather_fusion
  93.4 4.4 %scatter_fusion = f32[32,128,256]{2,1,0:T(8,128)} fusion(f32[32,128,256]{2,1,0:T(8,128)} %bitcast.206, s32[16]{0:T(128)S(1)} %fusion.55, f32[16,128,256]{2,1,0:T(8,128)S(1)} %copy.117), kind=kCustom, calls=%fused_computation.2.clone.clone.1 | custom fusion | flops 524288 | bytes 6291520 | tf_op jit(solution)/shard_map/while/body/eval_jaxpr/scatter-add | solution.py:94
  98.6 2.2 gather_fusion
  107.6 4.4 %scatter_fusion = f32[32,128,256]{2,1,0:T(8,128)} fusion(f32[32,128,256]{2,1,0:T(8,128)} %bitcast.206, s32[16]{0:T(128)S(1)} %fusion.55, f32[16,128,256]{2,1,0:T(8,128)S(1)} %copy.117), kind=kCustom, calls=%fused_computation.2.clone.clone.1 | custom fusion | flops 524288 | bytes 6291520 | tf_op jit(solution)/shard_map/while/body/eval_jaxpr/scatter-add | solution.py:94
  112.9 2.2 gather_fusion
  122.0 4.4 %scatter_fusion = f32[32,128,256]{2,1,0:T(8,128)} fusion(f32[32,128,256]{2,1,0:T(8,128)} %bitcast.206, s32[16]{0:T(128)S(1)} %fusion.55, f32[16,128,256]{2,1,0:T(8,128)S(1)} %copy.117), kind=kCustom, calls=%fused_computation.2.clone.clone.1 | custom fusion | flops 524288 | bytes 6291520 | tf_op jit(solution)/shard_map/while/body/eval_jaxpr/scatter-add | solution.py:94
  127.2 2.2 gather_fusion
  136.3 4.5 %scatter_fusion = f32[32,128,256]{2,1,0:T(8,128)} fusion(f32[32,128,256]{2,1,0:T(8,128)} %bitcast.206, s32[16]{0:T(128)S(1)} %fusion.55, f32[16,128,256]{2,1,0:T(8,128)S(1)} %copy.117), kind=kCustom, calls=%fused_computation.2.clone.clone.1 | custom fusion | flops 524288 | bytes 6291520 | tf_op jit(solution)/shard_map/while/body/eval_jaxpr/scatter-add | solution.py:94
  144.4 9.4 %collective-permute-start.2 = (bf16[1024,1,256]{2,0,1:T(8,128)(2,1)S(1)}, bf16[1024,1,256]{2,0,1:T(8,128)(2,1)S(1)}, u32[]{:S(2)}, u32[]{:S(2)}) collective-permute-start(bf16[1024,1,256]{2,0,1:T(8,128)(2,1)S(1)} %bitcast.212), channel_id=1, source_target_pairs={{0,64},{64,128},{128,192},{192,256},{256,320},{320,384},{384,448},... | collective-permute-start | bytes 1572872 | tf_op jit(solution)/shard_map/ppermute | solution.py:14
  154.3 2.1 reduce.4
  157.3 9.5 %all-to-all-start.1 = ((bf16[64,2,2048]{2,1,0:T(2,128)(2,1)}), bf16[64,2,2048]{2,1,0:T(2,128)(2,1)S(1)}, u32[]{:S(2)}, u32[]{:S(2)}) async-start(bf16[64,2,2048]{2,1,0:T(2,128)(2,1)} %reshape.448), calls=%async_computation.1 | async-start | bytes 1048576 | tf_op jit(solution)/shard_map/all_to_all | solution.py:120
  168.6 10.6 %collective-permute-done.3 = bf16[1024,1,256]{2,0,1:T(8,128)(2,1)S(1)} collective-permute-done((bf16[1024,1,256]{2,0,1:T(8,128)(2,1)S(1)}, bf16[1024,1,256]{2,0,1:T(8,128)(2,1)S(1)}, u32[]{:S(2)}, u32[]{:S(2)}) %collective-permute-start.3) | collective-permute-done | bytes 524320 | tf_op jit(solution)/shard_map/ppermute | solution.py:17
  181.8 8.1 %all-to-all-done.1 = bf16[64,2,2048]{2,1,0:T(2,128)(2,1)S(1)} async-done(((bf16[64,2,2048]{2,1,0:T(2,128)(2,1)}), bf16[64,2,2048]{2,1,0:T(2,128)(2,1)S(1)}, u32[]{:S(2)}, u32[]{:S(2)}) %all-to-all-start.1) | async-done | bytes 524320 | tf_op jit(solution)/shard_map/all_to_all | solution.py:120
  189.8 18.7 %all-to-all-start.2 = ((bf16[64,2,2048]{2,1,0:T(2,128)(2,1)}), bf16[64,2,2048]{2,1,0:T(2,128)(2,1)S(1)}, u32[]{:S(2)}, u32[]{:S(2)}) async-start(bf16[64,2,2048]{2,1,0:T(2,128)(2,1)} %reshape.450), calls=%async_computation.2 | async-start | bytes 1048576 | tf_op jit(solution)/shard_map/all_to_all | solution.py:121
  210.5 15.1 %all-to-all-done.2 = bf16[64,2,2048]{2,1,0:T(2,128)(2,1)S(1)} async-done(((bf16[64,2,2048]{2,1,0:T(2,128)(2,1)}), bf16[64,2,2048]{2,1,0:T(2,128)(2,1)S(1)}, u32[]{:S(2)}, u32[]{:S(2)}) %all-to-all-start.2) | async-done | bytes 524320 | tf_op jit(solution)/shard_map/all_to_all | solution.py:121
  225.6 6.1 %all-to-all-start.3 = ((bf16[64,2,2048]{2,1,0:T(2,128)(2,1)}), bf16[64,2,2048]{2,1,0:T(2,128)(2,1)S(1)}, u32[]{:S(2)}, u32[]{:S(2)}) async-start(bf16[64,2,2048]{2,1,0:T(2,128)(2,1)} %reshape.452), calls=%async_computation.3 | async-start | bytes 1048576 | tf_op jit(solution)/shard_map/all_to_all | solution.py:122
  235.3 13.6 %all-to-all-done.3 = bf16[64,2,2048]{2,1,0:T(2,128)(2,1)S(1)} async-done(((bf16[64,2,2048]{2,1,0:T(2,128)(2,1)}), bf16[64,2,2048]{2,1,0:T(2,128)(2,1)S(1)}, u32[]{:S(2)}, u32[]{:S(2)}) %all-to-all-start.3) | async-done | bytes 524320 | tf_op jit(solution)/shard_map/all_to_all | solution.py:122
  (132 shorter events, 53.4 us)
Async XLA Ops:
  0.6 16.1 %copy-start.1 = (bf16[2048,1,128]{2,0,1:T(8,128)(2,1)S(1)}, bf16[2048,1,128]{2,0,1:T(8,128)(2,1)}, u32[]{:S(2)}) copy-start(bf16[2048,1,128]{2,0,1:T(8,128)(2,1)} %param.10) | copy-start | bytes 1572868
  0.6 16.2 %copy-start.2 = (bf16[2048,1,128]{2,0,1:T(8,128)(2,1)S(1)}, bf16[2048,1,128]{2,0,1:T(8,128)(2,1)}, u32[]{:S(2)}) copy-start(bf16[2048,1,128]{2,0,1:T(8,128)(2,1)} %param.11) | copy-start | bytes 1572868
  3.3 76.8 %all-to-all-start = ((bf16[32,64,128]{2,0,1:T(8,128)(2,1)}), bf16[32,64,128]{2,0,1:T(8,128)(2,1)S(1)}, u32[]{:S(2)}, u32[]{:S(2)}) async-start(bf16[32,64,128]{2,0,1:T(8,128)(2,1)} %copy.79), calls=%async_computation | async-start | bytes 1048576 | tf_op jit(solution)/shard_map/all_to_all | solution.py:63
  16.7 8.1 %copy-start.5 = (s32[192]{0:T(256)S(1)}, s32[192]{0:T(256)}, u32[]{:S(2)}) copy-start(s32[192]{0:T(256)} %param.15) | copy-start | bytes 2308
  16.7 8.2 %copy-start.4 = (s32[192,4]{0,1:T(4,128)S(1)}, s32[192,4]{0,1:T(4,128)}, u32[]{:S(2)}) copy-start(s32[192,4]{0,1:T(4,128)} %param.14) | copy-start | bytes 9220
  17.1 19.1 %collective-permute-start = (bf16[1024,1,256]{2,0,1:T(8,128)(2,1)S(1)}, bf16[1024,1,256]{2,0,1:T(8,128)(2,1)}, u32[]{:S(2)}, u32[]{:S(2)}) collective-permute-start(bf16[1024,1,256]{2,0,1:T(8,128)(2,1)S(1)} %get-tuple-element.156), channel_id=1, source_target_pairs={{0,64},{64,128},{128,192},{192,256},{256,320},{320,384},{384,448},... | collective-permute-start | bytes 1572872 | tf_op jit(solution)/shard_map/ppermute | solution.py:14
  22.8 54.6 %collective-permute-start.1 = (bf16[1024,1,256]{2,0,1:T(8,128)(2,1)S(1)}, bf16[1024,1,256]{2,0,1:T(8,128)(2,1)}, u32[]{:S(2)}, u32[]{:S(2)}) collective-permute-start(bf16[1024,1,256]{2,0,1:T(8,128)(2,1)S(1)} %get-tuple-element.157), channel_id=1, source_target_pairs={{64,0},{128,64},{192,128},{256,192},{320,256},{384,320},{448,384},... | collective-permute-start | bytes 1572872 | tf_op jit(solution)/shard_map/ppermute | solution.py:17
  25.5 55.0 %copy-start.3 = (bf16[2048,1,128]{2,0,1:T(8,128)(2,1)S(1)}, bf16[2048,1,128]{2,0,1:T(8,128)(2,1)}, u32[]{:S(2)}) copy-start(bf16[2048,1,128]{2,0,1:T(8,128)(2,1)} %param.12) | copy-start | bytes 1572868
  81.0 2.4 copy-start
  142.5 36.7 %collective-permute-start.3 = (bf16[1024,1,256]{2,0,1:T(8,128)(2,1)S(1)}, bf16[1024,1,256]{2,0,1:T(8,128)(2,1)S(1)}, u32[]{:S(2)}, u32[]{:S(2)}) collective-permute-start(bf16[1024,1,256]{2,0,1:T(8,128)(2,1)S(1)} %bitcast.214), channel_id=1, source_target_pairs={{64,0},{128,64},{192,128},{256,192},{320,256},{384,320},{448,384},... | collective-permute-start | bytes 1572872 | tf_op jit(solution)/shard_map/ppermute | solution.py:17
  144.4 34.8 %collective-permute-start.2 = (bf16[1024,1,256]{2,0,1:T(8,128)(2,1)S(1)}, bf16[1024,1,256]{2,0,1:T(8,128)(2,1)S(1)}, u32[]{:S(2)}, u32[]{:S(2)}) collective-permute-start(bf16[1024,1,256]{2,0,1:T(8,128)(2,1)S(1)} %bitcast.212), channel_id=1, source_target_pairs={{0,64},{64,128},{128,192},{192,256},{256,320},{320,384},{384,448},... | collective-permute-start | bytes 1572872 | tf_op jit(solution)/shard_map/ppermute | solution.py:14
  157.3 32.5 %all-to-all-start.1 = ((bf16[64,2,2048]{2,1,0:T(2,128)(2,1)}), bf16[64,2,2048]{2,1,0:T(2,128)(2,1)S(1)}, u32[]{:S(2)}, u32[]{:S(2)}) async-start(bf16[64,2,2048]{2,1,0:T(2,128)(2,1)} %reshape.448), calls=%async_computation.1 | async-start | bytes 1048576 | tf_op jit(solution)/shard_map/all_to_all | solution.py:120
  189.8 35.8 %all-to-all-start.2 = ((bf16[64,2,2048]{2,1,0:T(2,128)(2,1)}), bf16[64,2,2048]{2,1,0:T(2,128)(2,1)S(1)}, u32[]{:S(2)}, u32[]{:S(2)}) async-start(bf16[64,2,2048]{2,1,0:T(2,128)(2,1)} %reshape.450), calls=%async_computation.2 | async-start | bytes 1048576 | tf_op jit(solution)/shard_map/all_to_all | solution.py:121
  225.6 23.2 %all-to-all-start.3 = ((bf16[64,2,2048]{2,1,0:T(2,128)(2,1)}), bf16[64,2,2048]{2,1,0:T(2,128)(2,1)S(1)}, u32[]{:S(2)}, u32[]{:S(2)}) async-start(bf16[64,2,2048]{2,1,0:T(2,128)(2,1)} %reshape.452), calls=%async_computation.3 | async-start | bytes 1048576 | tf_op jit(solution)/shard_map/all_to_all | solution.py:122
where the time goes:
time: 252 us; the launch traced here: 251 us
  waiting for transfers between devices  99.3 us (39%)
  starting transfers between devices  66.7 us (26%)
  local copies, waits for them, and re-layouts  40.2 us (16%)
  other arithmetic  33.5 us (13%)
  matrix products  9.61 us (4%)
    ppermute x2, waiting for transfers between devices, with_halo(): lax.ppermute(lax.slice_in_dim(block, 0, width, axis=dim), axis, backward)  51.8 us
    all_to_all x1, starting transfers between devices, per_device(): lax.all_to_all(grad_k, 'head', split_axis=0, concat_axis=1, tiled=True)  18.7 us
    scatter-add x4, other arithmetic, own_step(): totals.at[list_blk.reshape(-1)]  17.8 us
    ppermute x2, starting transfers between devices, with_halo(): lax.ppermute(lax.slice_in_dim(block, block.shape[dim] - width, None, axis...  15.1 us
    all_to_all x1, waiting for transfers between devices, per_device(): lax.all_to_all(grad_k, 'head', split_axis=0, concat_axis=1, tiled=True)  15.1 us
    all_to_all x1, waiting for transfers between devices, per_device(): lax.all_to_all(grad_v, 'head', split_axis=0, concat_axis=1, tiled=True)  13.6 us
    all_to_all x1, starting transfers between devices, per_device(): lax.all_to_all(out_grad.reshape(seq_rows, batch * width // head_dim, head...  13.5 us
    ppermute x2, waiting for transfers between devices, with_halo(): lax.ppermute(lax.slice_in_dim(block, block.shape[dim] - width, None, axis...  10.7 us
  transfers between devices with their start and end apart: 8, of which 6 were waited for; matrix products, arithmetic and copies ran while one was open for 7% of the time, Pallas kernels for 0%

commit v1 on v0

v1 whole, which is shorter than its diff:
```python
import jax
import jax.numpy as jnp
from jax import lax
from jax.experimental import pallas as pl
from jax.experimental.pallas import tpu as pltpu
from jax.sharding import PartitionSpec as P

TILE = 128
NT = (((1,), (1,)), ((), ()))
NN = (((1,), (0,)), ((), ()))
TN = (((0,), (0,)), ((), ()))


def attend_kernel(tiles_dev, nbr_count, ring_len):
    half = tiles_dev // 2 * TILE
    own = tiles_dev * TILE

    def kernel(
        shard, nbr, cnt, q_any, k_any, v_any, o_any, g_any, klo, khi, vlo, vhi, vz,
        dq_ref, mid_k, mid_v, dk_lo, dk_hi, dv_lo, dv_hi,
        q, o, g, k_ext, v_ext, dk_acc, dv_acc, sems,
    ):
        s = shard[0]
        first_tile = s * tiles_dev
        ext_base = first_tile - tiles_dev // 2
        col = lax.rem(s, ring_len)

        def load(src, dst, i):
            pltpu.make_async_copy(src, dst, sems.at[i]).start()

        load(k_any, k_ext.at[pl.ds(half, own)], 0)
        load(v_any, v_ext.at[pl.ds(half, own)], 1)
        load(q_any, q, 2)
        load(o_any, o, 3)
        load(g_any, g, 4)
        load(klo, k_ext.at[pl.ds(0, half)], 5)
        load(khi, k_ext.at[pl.ds(half + own, half)], 6)
        v_low = v_ext.at[pl.ds(0, half)]
        v_high = v_ext.at[pl.ds(half + own, half)]

        @pl.when(col == 0)
        def _():
            load(vz, v_low, 7)

        @pl.when(col != 0)
        def _():
            load(vlo, v_low, 7)

        @pl.when(col == ring_len - 1)
        def _():
            load(vz, v_high, 8)

        @pl.when(col != ring_len - 1)
        def _():
            load(vhi, v_high, 8)

        dk_acc[...] = jnp.zeros_like(dk_acc)
        dv_acc[...] = jnp.zeros_like(dv_acc)
        for src, dst, i in (
            (k_any, k_ext.at[pl.ds(half, own)], 0),
            (v_any, v_ext.at[pl.ds(half, own)], 1),
            (q_any, q, 2),
            (o_any, o, 3),
            (g_any, g, 4),
            (klo, k_ext.at[pl.ds(0, half)], 5),
            (khi, k_ext.at[pl.ds(half + own, half)], 6),
            (vlo, v_low, 7),
            (vhi, v_high, 8),
        ):
            pltpu.make_async_copy(src, dst, sems.at[i]).wait()
        rows = lax.broadcasted_iota(jnp.int32, (TILE, TILE), 0)
        scale = TILE ** (-0.5)

        def step(t, carry):
            at = pl.ds(pl.multiple_of(t * TILE, TILE), TILE)
            tile = first_tile + t
            q_t = q[at, :]
            g_t = jnp.where(rows < cnt[tile], g[at, :].astype(jnp.float32), 0.0)
            delta = jnp.sum((g_t * o[at, :].astype(jnp.float32)).T, axis=0, keepdims=True)
            g_t = g_t.astype(jnp.bfloat16)
            places, keys, scores = [], [], []
            for n in range(nbr_count):
                near = nbr[tile * nbr_count + n]
                place = pl.ds(pl.multiple_of((near - ext_base) * TILE, TILE), TILE)
                key = k_ext[place, :]
                score = lax.dot_general(key, q_t, NT, preferred_element_type=jnp.float32) * scale
                places.append(place)
                keys.append(key)
                scores.append(jnp.where(rows < cnt[near], score, -jnp.inf))
            top = scores[0]
            for score in scores[1:]:
                top = jnp.maximum(top, score)
            top = jnp.max(top, axis=0, keepdims=True)
            probs = [jnp.exp(score - top) for score in scores]
            total = probs[0]
            for prob in probs[1:]:
                total = total + prob
            inv = 1.0 / jnp.sum(total, axis=0, keepdims=True)
            dq = jnp.zeros((TILE, TILE), jnp.float32)
            for place, key, prob in zip(places, keys, probs):
                prob = prob * inv
                dprob = lax.dot_general(
                    v_ext[place, :], g_t, NT, preferred_element_type=jnp.float32
                )
                dscore = (prob * (dprob - delta) * scale).astype(jnp.bfloat16)
                dq = dq + lax.dot_general(dscore, key, TN, preferred_element_type=jnp.float32)
                dk_acc[place, :] += lax.dot_general(
                    dscore, q_t, NN, preferred_element_type=jnp.float32
                )
                dv_acc[place, :] += lax.dot_general(
                    prob.astype(jnp.bfloat16), g_t, NN, preferred_element_type=jnp.float32
                )
            dq_ref[at, :] = dq.astype(jnp.bfloat16)
            return carry

        lax.fori_loop(0, tiles_dev, step, 0)
        mid_k[...] = dk_acc[pl.ds(half, own), :]
        mid_v[...] = dv_acc[pl.ds(half, own), :]
        dk_lo[...] = dk_acc[pl.ds(0, half), :].astype(jnp.bfloat16)
        dk_hi[...] = dk_acc[pl.ds(half + own, half), :].astype(jnp.bfloat16)
        dv_lo[...] = dv_acc[pl.ds(0, half), :].astype(jnp.bfloat16)
        dv_hi[...] = dv_acc[pl.ds(half + own, half), :].astype(jnp.bfloat16)

    return kernel


def combine_kernel(peers, share, ring_len):
    half_peers = peers // 2

    def kernel(shard, mid_k, mid_v, k_low, k_high, v_low, v_high, v_far, out):
        col = lax.rem(shard[0], ring_len)
        mk = mid_k[...].reshape(peers, share, TILE)
        mv = mid_v[...].reshape(peers, share, TILE)
        far = v_far[...]
        back = (
            (mk[:half_peers], k_low[...], 0, 0),
            (mk[half_peers:], k_high[...], 0, half_peers),
            (mv[:half_peers], jnp.where(col == 0, far, v_low[...]), 1, 0),
            (mv[half_peers:], jnp.where(col == ring_len - 1, far, v_high[...]), 1, half_peers),
        )
        for mid, term, which, start in back:
            total = mid + term.astype(jnp.float32).reshape(half_peers, share, TILE)
            out[pl.ds(start, half_peers), which] = total.astype(jnp.bfloat16)

    return kernel


def routes(seq_count, ring_len):
    rings = seq_count // ring_len
    forward = [(i, i + 1) for i in range(seq_count - 1)]
    around = [
        (r * ring_len + x, r * ring_len + (x + 1) % ring_len)
        for r in range(rings)
        for x in range(ring_len)
    ]
    across = [(r * ring_len, (r + 1) * ring_len) for r in range(rings - 1)] + [
        ((r + 1) * ring_len - 1, r * ring_len - 1) for r in range(1, rings)
    ]
    return forward, around, across


def per_device(query_rows, key_rows, value_rows, attn_output, out_grad, neighbours, counts):
    seq_rows, batch, width = out_grad.shape
    shard_tokens, _, head_dim = query_rows.shape
    nbr_count = neighbours.shape[1]
    tiles_dev = shard_tokens // TILE
    half = shard_tokens // 2
    peers = shard_tokens // seq_rows
    seq_count = lax.axis_size("seq")
    ring_len = 4 if seq_count % 4 == 0 else seq_count
    forward, around, across = routes(seq_count, ring_len)
    backward = [(b, a) for a, b in forward]
    around_back = [(b, a) for a, b in around]
    shard = lax.axis_index("seq").astype(jnp.int32)
    at_start = lax.rem(shard, ring_len) == 0

    def exchange(low, high):
        ring_low = lax.ppermute(high, "seq", around)
        ring_high = lax.ppermute(low, "seq", around_back)
        far = lax.ppermute(jnp.where(at_start, ring_low, ring_high), "seq", across)
        return ring_low, ring_high, far

    q = query_rows.reshape(shard_tokens, head_dim)
    k = key_rows.reshape(shard_tokens, head_dim)
    v = value_rows.reshape(shard_tokens, head_dim)
    o = attn_output.reshape(shard_tokens, head_dim)
    v_low, v_high, v_far = exchange(v[:half], v[half:])
    k_low = lax.ppermute(k[half:], "seq", forward)
    k_high = lax.ppermute(k[:half], "seq", backward)
    grads = lax.all_to_all(
        out_grad.reshape(seq_rows, peers, head_dim),
        "head",
        split_axis=1,
        concat_axis=0,
        tiled=True,
    ).reshape(shard_tokens, head_dim)

    smem = pl.BlockSpec(memory_space=pltpu.SMEM)
    vmem = pl.BlockSpec(memory_space=pltpu.VMEM)
    hbm = pl.BlockSpec(memory_space=pl.ANY)
    rows = jax.ShapeDtypeStruct((shard_tokens, head_dim), jnp.bfloat16)
    mid = jax.ShapeDtypeStruct((shard_tokens, head_dim), jnp.float32)
    flank = jax.ShapeDtypeStruct((half, head_dim), jnp.bfloat16)
    dq, mid_k, mid_v, dk_low, dk_high, dv_low, dv_high = pl.pallas_call(
        attend_kernel(tiles_dev, nbr_count, ring_len),
        out_shape=(rows, mid, mid, flank, flank, flank, flank),
        in_specs=[smem] * 3 + [hbm] * 10,
        out_specs=(vmem,) * 7,
        scratch_shapes=[
            pltpu.VMEM((shard_tokens, head_dim), jnp.bfloat16),
            pltpu.VMEM((shard_tokens, head_dim), jnp.bfloat16),
            pltpu.VMEM((shard_tokens, head_dim), jnp.bfloat16),
            pltpu.VMEM((2 * shard_tokens, head_dim), jnp.bfloat16),
            pltpu.VMEM((2 * shard_tokens, head_dim), jnp.bfloat16),
            pltpu.VMEM((2 * shard_tokens, head_dim), jnp.float32),
            pltpu.VMEM((2 * shard_tokens, head_dim), jnp.float32),
            pltpu.SemaphoreType.DMA((9,)),
        ],
        name="attend",
    )(
        shard.reshape(1), neighbours.reshape(-1), counts,
        q, k, v, o, grads, k_low, k_high, v_low, v_high, v_far,
    )
    rv_low, rv_high, rv_far = exchange(dv_low, dv_high)
    rk_low = lax.ppermute(dk_high, "seq", forward)
    rk_high = lax.ppermute(dk_low, "seq", backward)
    back_q = lax.all_to_all(
        dq.reshape(peers, seq_rows, head_dim), "head", split_axis=0, concat_axis=0, tiled=True
    )
    joint = pl.pallas_call(
        combine_kernel(peers, seq_rows, ring_len),
        out_shape=jax.ShapeDtypeStruct((peers, 2, seq_rows, head_dim), jnp.bfloat16),
        in_specs=[smem] + [vmem] * 7,
        out_specs=vmem,
        name="combine",
    )(shard.reshape(1), mid_k, mid_v, rk_low, rk_high, rv_low, rv_high, rv_far)
    back_kv = lax.all_to_all(joint, "head", split_axis=0, concat_axis=0, tiled=True)

    def to_rows(block):
        return block.transpose(1, 0, 2).reshape(seq_rows, batch, width)

    return to_rows(back_q), to_rows(back_kv[:, 0]), to_rows(back_kv[:, 1])


def solution(mesh):
    placed = (
        P("seq", "head", None),
        P("seq", "head", None),
        P("seq", "head", None),
        P("seq", "head", None),
        P(("seq", "head"), None, None),
        P(),
        P(),
    )
    return jax.shard_map(
        per_device,
        mesh=mesh,
        in_specs=placed,
        out_specs=(
            P(("seq", "head"), None, None),
            P(("seq", "head"), None, None),
            P(("seq", "head"), None, None),
        ),
        check_vma=False,
    )
```

time: 252 us -> 193 us (0.77)
  the two profiles are of different devices: /device:TPU:263 before, /device:TPU:1 now
where the time goes in v1:
time: 193 us
  starting transfers between devices  119 us (62%)
  waiting for transfers between devices  40.7 us (21%)
  Pallas kernels  22.2 us (12%)
  local copies, waits for them, and re-layouts  9.77 us (5%)
    all_to_all x1, starting transfers between devices, per_device(): lax.all_to_all(dq.reshape(peers, seq_rows, head_dim), 'head', split_axis=...  29.5 us
    all_to_all x1, starting transfers between devices, per_device(): lax.all_to_all(joint, 'head', split_axis=0, concat_axis=0, tiled=True)  28.9 us
    all_to_all x1, waiting for transfers between devices, per_device(): lax.all_to_all(joint, 'head', split_axis=0, concat_axis=0, tiled=True)  27.5 us
    ppermute x2, starting transfers between devices, exchange(): far = lax.ppermute(jnp.where(at_start, ring_low, ring_high), 'seq', across)  23.9 us
    pallas_call x1, Pallas kernels, per_device(): pl.pallas_call(attend_kernel(tiles_dev, nbr_count, ring_len), out_shape=(...  19.1 us
    all_to_all x1, starting transfers between devices, per_device(): lax.all_to_all(out_grad.reshape(seq_rows, peers, head_dim), 'head', split...  14.7 us
    ppermute x2, starting transfers between devices, exchange(): ring_high = lax.ppermute(low, 'seq', around_back)  10.3 us
    ppermute x2, waiting for transfers between devices, exchange(): far = lax.ppermute(jnp.where(at_start, ring_low, ring_high), 'seq', across)  7.72 us
  transfers between devices with their start and end apart: 13, of which 6 were waited for; matrix products, arithmetic and copies ran while one was open for 1% of the time, Pallas kernels for 2%

profile of v1, /device:TPU:1, one launch (start us, length us, event | category | flops | bytes accessed | tf_op | source)
XLA Modules:
  0.0 192.8 jit_solution(5011863073725909152)
XLA Ops:
  0.6 1.4 reshape.54
  2.0 1.1 copy.13
  3.1 14.7 %all-to-all-start = ((bf16[32,64,128]{2,0,1:T(8,128)(2,1)}), bf16[32,64,128]{2,0,1:T(8,128)(2,1)S(1)}, u32[]{:S(2)}, u32[]{:S(2)}) async-start(bf16[32,64,128]{2,0,1:T(8,128)(2,1)} %copy.13), calls=%async_computation | async-start | bytes 1048576 | tf_op jit(solution)/shard_map/all_to_all | solution.py:190
  17.9 4.5 %collective-permute-start.3 = (bf16[1024,128]{1,0:T(8,128)(2,1)S(1)}, bf16[1024,128]{1,0:T(8,128)(2,1)S(1)}, u32[]{:S(2)}, u32[]{:S(2)}) collective-permute-start(bf16[1024,128]{1,0:T(8,128)(2,1)S(1)} %get-tuple-element.19), channel_id=1, source_target_pairs={{64,0},{128,64},{192,128},{0,192},{320,256},{384,320},{448,384},{2... | collective-permute-start | bytes 786440 | tf_op jit(solution)/shard_map/ppermute | solution.py:179
  22.5 1.9 collective-permute-start.2
  24.4 1.3 collective-permute-start.1
  25.7 4.0 %collective-permute-start = (bf16[1024,128]{1,0:T(8,128)(2,1)S(1)}, bf16[1024,128]{1,0:T(8,128)(2,1)S(1)}, u32[]{:S(2)}, u32[]{:S(2)}) collective-permute-start(bf16[1024,128]{1,0:T(8,128)(2,1)S(1)} %get-tuple-element.22), channel_id=1, source_target_pairs={{0,64},{64,128},{128,192},{192,256},{256,320},{320,384},{384,448},... | collective-permute-start | bytes 786440 | tf_op jit(solution)/shard_map/ppermute | solution.py:188
  29.8 2.9 %collective-permute-done.2.vlo = bf16[1024,128]{1,0:T(8,128)(2,1)S(1)} collective-permute-done((bf16[1024,128]{1,0:T(8,128)(2,1)S(1)}, bf16[1024,128]{1,0:T(8,128)(2,1)S(1)}, u32[]{:S(2)}, u32[]{:S(2)}) %collective-permute-start.2) | collective-permute-done | bytes 262176 | tf_op jit(solution)/shard_map/ppermute | solution.py:178
  33.4 10.3 %collective-permute-start.4 = (bf16[1024,128]{1,0:T(8,128)(2,1)S(1)}, bf16[1024,128]{1,0:T(8,128)(2,1)S(1)}, u32[]{:S(2)}, u32[]{:S(2)}) collective-permute-start(bf16[1024,128]{1,0:T(8,128)(2,1)S(1)} %broadcast_select_fusion.1), channel_id=1, source_target_pairs={{0,256},{256,512},{448,192},{704,448},{1,257},{257,513},{449,193},... | collective-permute-start | bytes 786440 | tf_op jit(solution)/shard_map/ppermute | solution.py:180
  44.6 3.3 %collective-permute-done.4.vz = bf16[1024,128]{1,0:T(8,128)(2,1)S(1)} collective-permute-done((bf16[1024,128]{1,0:T(8,128)(2,1)S(1)}, bf16[1024,128]{1,0:T(8,128)(2,1)S(1)}, u32[]{:S(2)}, u32[]{:S(2)}) %collective-permute-start.4) | collective-permute-done | bytes 262176 | tf_op jit(solution)/shard_map/ppermute | solution.py:180
  48.8 19.1 %attend.1 = (bf16[2048,128]{1,0:T(8,128)(2,1)}, f32[2048,128]{1,0:T(8,128)}, f32[2048,128]{1,0:T(8,128)}, bf16[1024,128]{1,0:T(8,128)(2,1)}, bf16[1024,128]{1,0:...) custom-call(s32[1]{0:T(128)} %bitcast.shard, s32[768]{0:T(1024)} %reshape.49.nbr, s32[192]{0:T(256)} %cnt.1, ...), custom_call_target="tpu_custom_call" | custom-call | tf_op jit(solution)/shard_map/attend/pallas_call | solution.py:204
  67.9 29.5 %all-to-all-start.1 = ((bf16[64,32,128]{2,1,0:T(8,128)(2,1)}), bf16[64,32,128]{2,1,0:T(8,128)(2,1)S(1)}, u32[]{:S(2)}, u32[]{:S(2)}) async-start(bf16[64,32,128]{2,1,0:T(8,128)(2,1)} %bitcast.34), calls=%async_computation.1 | async-start | bytes 1048576 | tf_op jit(solution)/shard_map/all_to_all | solution.py:227
  97.4 1.9 collective-permute-start.7
  99.3 5.8 %collective-permute-start.8 = (bf16[1024,128]{1,0:T(8,128)(2,1)S(1)}, bf16[1024,128]{1,0:T(8,128)(2,1)S(1)}, u32[]{:S(2)}, u32[]{:S(2)}) collective-permute-start(bf16[1024,128]{1,0:T(8,128)(2,1)S(1)} %copy-done.16), channel_id=1, source_target_pairs={{64,0},{128,64},{192,128},{0,192},{320,256},{384,320},{448,384},{2... | collective-permute-start | bytes 786440 | tf_op jit(solution)/shard_map/ppermute | solution.py:179
  105.1 1.3 collective-permute-start.5
  106.4 1.3 collective-permute-start.6
  107.7 1.6 collective-permute-done.7.v_low
  111.0 13.6 %collective-permute-start.9 = (bf16[1024,128]{1,0:T(8,128)(2,1)S(1)}, bf16[1024,128]{1,0:T(8,128)(2,1)S(1)}, u32[]{:S(2)}, u32[]{:S(2)}) collective-permute-start(bf16[1024,128]{1,0:T(8,128)(2,1)S(1)} %broadcast_select_fusion), channel_id=1, source_target_pairs={{0,256},{256,512},{448,192},{704,448},{1,257},{257,513},{449,193},... | collective-permute-start | bytes 786440 | tf_op jit(solution)/shard_map/ppermute | solution.py:180
  124.6 4.4 %collective-permute-done.9.v_far = bf16[1024,128]{1,0:T(8,128)(2,1)S(1)} collective-permute-done((bf16[1024,128]{1,0:T(8,128)(2,1)S(1)}, bf16[1024,128]{1,0:T(8,128)(2,1)S(1)}, u32[]{:S(2)}, u32[]{:S(2)}) %collective-permute-start.9) | collective-permute-done | bytes 262176 | tf_op jit(solution)/shard_map/ppermute | solution.py:180
  129.7 3.1 %combine.1 = bf16[64,2,32,128]{3,2,1,0:T(8,128)(2,1)} custom-call(s32[1]{0:T(128)} %bitcast.shard, f32[2048,128]{1,0:T(8,128)} %get-tuple-element.11.mid_k, f32[2048,128]{1,0:T(8,128)} %get-tuple-element.12.mid_v, bf16[1024,128]{1,0:T(8,128)(2,1)} %copy-done.7, bf16[1024,128]{1,0:T(8,128)(2,1)} %copy-done.8, bf16[1024,128]{1,0:T(8,128)(2,1)} %copy-done.3, ...), custom_call_target="tpu_custom_call" | custom-call | tf_op jit(solution)/shard_map/combine/pallas_call | solution.py:230
  132.8 28.9 %all-to-all-start.2 = ((bf16[64,2,32,128]{3,2,1,0:T(8,128)(2,1)}), bf16[64,2,32,128]{3,2,1,0:T(8,128)(2,1)S(1)}, u32[]{:S(2)}, u32[]{:S(2)}) async-start(bf16[64,2,32,128]{3,2,1,0:T(8,128)(2,1)} %combine.1), calls=%async_computation.2 | async-start | bytes 2097152 | tf_op jit(solution)/shard_map/all_to_all | solution.py:237
  162.0 0.9 reshape.57
  162.9 27.5 %all-to-all-done.2 = bf16[64,2,32,128]{3,2,1,0:T(8,128)(2,1)S(1)} async-done(((bf16[64,2,32,128]{3,2,1,0:T(8,128)(2,1)}), bf16[64,2,32,128]{3,2,1,0:T(8,128)(2,1)S(1)}, u32[]{:S(2)}, u32[]{:S(2)}) %all-to-all-start.2) | async-done | bytes 1048608 | tf_op jit(solution)/shard_map/all_to_all | solution.py:237
  191.8 0.9 reshape.58
  (55 shorter events, 6.4 us)
Async XLA Ops:
  3.1 14.7 %copy-start.1 = (bf16[2048,1,128]{2,0,1:T(8,128)(2,1)S(1)}, bf16[2048,1,128]{2,0,1:T(8,128)(2,1)}, u32[]{:S(2)}) copy-start(bf16[2048,1,128]{2,0,1:T(8,128)(2,1)} %param.9) | copy-start | bytes 1572868
  3.1 44.8 %all-to-all-start = ((bf16[32,64,128]{2,0,1:T(8,128)(2,1)}), bf16[32,64,128]{2,0,1:T(8,128)(2,1)S(1)}, u32[]{:S(2)}, u32[]{:S(2)}) async-start(bf16[32,64,128]{2,0,1:T(8,128)(2,1)} %copy.13), calls=%async_computation | async-start | bytes 1048576 | tf_op jit(solution)/shard_map/all_to_all | solution.py:190
  17.9 6.5 %copy-start = (bf16[2048,1,128]{2,0,1:T(8,128)(2,1)S(1)}, bf16[2048,1,128]{2,0,1:T(8,128)(2,1)}, u32[]{:S(2)}) copy-start(bf16[2048,1,128]{2,0,1:T(8,128)(2,1)} %param.8) | copy-start | bytes 1572868
  17.9 11.8 %collective-permute-start.3 = (bf16[1024,128]{1,0:T(8,128)(2,1)S(1)}, bf16[1024,128]{1,0:T(8,128)(2,1)S(1)}, u32[]{:S(2)}, u32[]{:S(2)}) collective-permute-start(bf16[1024,128]{1,0:T(8,128)(2,1)S(1)} %get-tuple-element.19), channel_id=1, source_target_pairs={{64,0},{128,64},{192,128},{0,192},{320,256},{384,320},{448,384},{2... | collective-permute-start | bytes 786440 | tf_op jit(solution)/shard_map/ppermute | solution.py:179
  22.5 10.2 %collective-permute-start.2 = (bf16[1024,128]{1,0:T(8,128)(2,1)S(1)}, bf16[1024,128]{1,0:T(8,128)(2,1)S(1)}, u32[]{:S(2)}, u32[]{:S(2)}) collective-permute-start(bf16[1024,128]{1,0:T(8,128)(2,1)S(1)} %get-tuple-element.20), channel_id=1, source_target_pairs={{0,64},{64,128},{128,192},{192,0},{256,320},{320,384},{384,448},{4... | collective-permute-start | bytes 786440 | tf_op jit(solution)/shard_map/ppermute | solution.py:178
  24.4 20.2 %collective-permute-start.1 = (bf16[1024,128]{1,0:T(8,128)(2,1)S(1)}, bf16[1024,128]{1,0:T(8,128)(2,1)S(1)}, u32[]{:S(2)}, u32[]{:S(2)}) collective-permute-start(bf16[1024,128]{1,0:T(8,128)(2,1)S(1)} %get-tuple-element.21), channel_id=1, source_target_pairs={{64,0},{128,64},{192,128},{256,192},{320,256},{384,320},{448,384},... | collective-permute-start | bytes 786440 | tf_op jit(solution)/shard_map/ppermute | solution.py:189
  25.7 18.9 %collective-permute-start = (bf16[1024,128]{1,0:T(8,128)(2,1)S(1)}, bf16[1024,128]{1,0:T(8,128)(2,1)S(1)}, u32[]{:S(2)}, u32[]{:S(2)}) collective-permute-start(bf16[1024,128]{1,0:T(8,128)(2,1)S(1)} %get-tuple-element.22), channel_id=1, source_target_pairs={{0,64},{64,128},{128,192},{192,256},{256,320},{320,384},{384,448},... | collective-permute-start | bytes 786440 | tf_op jit(solution)/shard_map/ppermute | solution.py:188
  29.8 14.0 %copy-start.13 = (s32[192,4]{0,1:T(4,128)S(1)}, s32[192,4]{0,1:T(4,128)}, u32[]{:S(2)}) copy-start(s32[192,4]{0,1:T(4,128)} %param.12) | copy-start | bytes 9220
  33.4 14.5 %collective-permute-start.4 = (bf16[1024,128]{1,0:T(8,128)(2,1)S(1)}, bf16[1024,128]{1,0:T(8,128)(2,1)S(1)}, u32[]{:S(2)}, u32[]{:S(2)}) collective-permute-start(bf16[1024,128]{1,0:T(8,128)(2,1)S(1)} %broadcast_select_fusion.1), channel_id=1, source_target_pairs={{0,256},{256,512},{448,192},{704,448},{1,257},{257,513},{449,193},... | collective-permute-start | bytes 786440 | tf_op jit(solution)/shard_map/ppermute | solution.py:180
  44.6 3.3 %copy-start.10 = (bf16[1024,128]{1,0:T(8,128)(2,1)}, bf16[1024,128]{1,0:T(8,128)(2,1)S(1)}, u32[]{:S(2)}) copy-start(bf16[1024,128]{1,0:T(8,128)(2,1)S(1)} %collective-permute-done.1.khi) | copy-start | bytes 786436
  44.6 3.3 %copy-start.11 = (bf16[1024,128]{1,0:T(8,128)(2,1)}, bf16[1024,128]{1,0:T(8,128)(2,1)S(1)}, u32[]{:S(2)}) copy-start(bf16[1024,128]{1,0:T(8,128)(2,1)S(1)} %collective-permute-done.klo) | copy-start | bytes 786436
  67.9 29.5 %copy-start.17 = (bf16[1024,128]{1,0:T(8,128)(2,1)S(1)}, bf16[1024,128]{1,0:T(8,128)(2,1)}, u32[]{:S(2)}) copy-start(bf16[1024,128]{1,0:T(8,128)(2,1)} %get-tuple-element.15) | copy-start | bytes 786436
  67.9 31.4 %copy-start.16 = (bf16[1024,128]{1,0:T(8,128)(2,1)S(1)}, bf16[1024,128]{1,0:T(8,128)(2,1)}, u32[]{:S(2)}) copy-start(bf16[1024,128]{1,0:T(8,128)(2,1)} %get-tuple-element.16) | copy-start | bytes 786436
  67.9 37.2 %copy-start.15 = (bf16[1024,128]{1,0:T(8,128)(2,1)S(1)}, bf16[1024,128]{1,0:T(8,128)(2,1)}, u32[]{:S(2)}) copy-start(bf16[1024,128]{1,0:T(8,128)(2,1)} %get-tuple-element.13) | copy-start | bytes 786436
  67.9 38.5 %copy-start.14 = (bf16[1024,128]{1,0:T(8,128)(2,1)S(1)}, bf16[1024,128]{1,0:T(8,128)(2,1)}, u32[]{:S(2)}) copy-start(bf16[1024,128]{1,0:T(8,128)(2,1)} %get-tuple-element.14) | copy-start | bytes 786436
  67.9 64.9 %all-to-all-start.1 = ((bf16[64,32,128]{2,1,0:T(8,128)(2,1)}), bf16[64,32,128]{2,1,0:T(8,128)(2,1)S(1)}, u32[]{:S(2)}, u32[]{:S(2)}) async-start(bf16[64,32,128]{2,1,0:T(8,128)(2,1)} %bitcast.34), calls=%async_computation.1 | async-start | bytes 1048576 | tf_op jit(solution)/shard_map/all_to_all | solution.py:227
  97.4 12.0 %collective-permute-start.7 = (bf16[1024,128]{1,0:T(8,128)(2,1)S(1)}, bf16[1024,128]{1,0:T(8,128)(2,1)S(1)}, u32[]{:S(2)}, u32[]{:S(2)}) collective-permute-start(bf16[1024,128]{1,0:T(8,128)(2,1)S(1)} %copy-done.17), channel_id=1, source_target_pairs={{0,64},{64,128},{128,192},{192,0},{256,320},{320,384},{384,448},{4... | collective-permute-start | bytes 786440 | tf_op jit(solution)/shard_map/ppermute | solution.py:178
  99.3 10.9 %collective-permute-start.8 = (bf16[1024,128]{1,0:T(8,128)(2,1)S(1)}, bf16[1024,128]{1,0:T(8,128)(2,1)S(1)}, u32[]{:S(2)}, u32[]{:S(2)}) collective-permute-start(bf16[1024,128]{1,0:T(8,128)(2,1)S(1)} %copy-done.16), channel_id=1, source_target_pairs={{64,0},{128,64},{192,128},{0,192},{320,256},{384,320},{448,384},{2... | collective-permute-start | bytes 786440 | tf_op jit(solution)/shard_map/ppermute | solution.py:179
  105.1 19.5 %collective-permute-start.5 = (bf16[1024,128]{1,0:T(8,128)(2,1)S(1)}, bf16[1024,128]{1,0:T(8,128)(2,1)S(1)}, u32[]{:S(2)}, u32[]{:S(2)}) collective-permute-start(bf16[1024,128]{1,0:T(8,128)(2,1)S(1)} %copy-done.15), channel_id=1, source_target_pairs={{0,64},{64,128},{128,192},{192,256},{256,320},{320,384},{384,448},... | collective-permute-start | bytes 786440 | tf_op jit(solution)/shard_map/ppermute | solution.py:225
  106.4 18.2 %collective-permute-start.6 = (bf16[1024,128]{1,0:T(8,128)(2,1)S(1)}, bf16[1024,128]{1,0:T(8,128)(2,1)S(1)}, u32[]{:S(2)}, u32[]{:S(2)}) collective-permute-start(bf16[1024,128]{1,0:T(8,128)(2,1)S(1)} %copy-done.14), channel_id=1, source_target_pairs={{64,0},{128,64},{192,128},{256,192},{320,256},{384,320},{448,384},... | collective-permute-start | bytes 786440 | tf_op jit(solution)/shard_map/ppermute | solution.py:226
  111.0 18.0 %collective-permute-start.9 = (bf16[1024,128]{1,0:T(8,128)(2,1)S(1)}, bf16[1024,128]{1,0:T(8,128)(2,1)S(1)}, u32[]{:S(2)}, u32[]{:S(2)}) collective-permute-start(bf16[1024,128]{1,0:T(8,128)(2,1)S(1)} %broadcast_select_fusion), channel_id=1, source_target_pairs={{0,256},{256,512},{448,192},{704,448},{1,257},{257,513},{449,193},... | collective-permute-start | bytes 786440 | tf_op jit(solution)/shard_map/ppermute | solution.py:180
  124.6 4.5 %copy-start.7 = (bf16[1024,128]{1,0:T(8,128)(2,1)}, bf16[1024,128]{1,0:T(8,128)(2,1)S(1)}, u32[]{:S(2)}) copy-start(bf16[1024,128]{1,0:T(8,128)(2,1)S(1)} %collective-permute-done.5.k_low) | copy-start | bytes 786436
  124.6 4.4 %copy-start.8 = (bf16[1024,128]{1,0:T(8,128)(2,1)}, bf16[1024,128]{1,0:T(8,128)(2,1)S(1)}, u32[]{:S(2)}) copy-start(bf16[1024,128]{1,0:T(8,128)(2,1)S(1)} %collective-permute-done.6.k_high) | copy-start | bytes 786436
  132.8 57.6 %all-to-all-start.2 = ((bf16[64,2,32,128]{3,2,1,0:T(8,128)(2,1)}), bf16[64,2,32,128]{3,2,1,0:T(8,128)(2,1)S(1)}, u32[]{:S(2)}, u32[]{:S(2)}) async-start(bf16[64,2,32,128]{3,2,1,0:T(8,128)(2,1)} %combine.1), calls=%async_computation.2 | async-start | bytes 2097152 | tf_op jit(solution)/shard_map/all_to_all | solution.py:237
  (7 other events, 7.6 us)

commit v2 on v1

v2 whole, which is shorter than its diff:
```python
import math

import jax
import jax.numpy as jnp
from jax import lax
from jax.experimental import pallas as pl
from jax.experimental.pallas import tpu as pltpu
from jax.sharding import PartitionSpec as P

TILE = 128
NT = (((1,), (1,)), ((), ()))
NN = (((1,), (0,)), ((), ()))
TN = (((0,), (0,)), ((), ()))


def dot(a, b, dims):
    return lax.dot_general(a, b, dims, preferred_element_type=jnp.float32)


def own_kernel(tiles_dev, nbr_count, ring_len):
    half_tiles = tiles_dev // 2
    half = half_tiles * TILE
    own = tiles_dev * TILE
    scale = TILE ** (-0.5)
    scale_two = scale * math.log2(math.e)

    def kernel(
        shard, nbr, cnt, q_any, k_any, v_any, o_any, g_any, klo, khi, vlo, vhi, vz,
        dq_ref, dk_ref, dv_ref, stat_lo, stat_hi,
        q, o, g, k_ext, v_ext, dk_acc, dv_acc, stats, p_even, p_odd, sems,
    ):
        s = shard[0]
        first_tile = s * tiles_dev
        ext_base = first_tile - half_tiles
        col = lax.rem(s, ring_len)
        v_low = v_ext.at[pl.ds(0, half)]
        v_high = v_ext.at[pl.ds(half + own, half)]
        moves = [
            (k_any, k_ext.at[pl.ds(half, own)]),
            (v_any, v_ext.at[pl.ds(half, own)]),
            (q_any, q),
            (o_any, o),
            (g_any, g),
            (klo, k_ext.at[pl.ds(0, half)]),
            (khi, k_ext.at[pl.ds(half + own, half)]),
            (vlo, v_low),
            (vhi, v_high),
        ]

        def load(i, src=None):
            source = moves[i][0] if src is None else src
            pltpu.make_async_copy(source, moves[i][1], sems.at[i]).start()

        for i in range(7):
            load(i)
        pl.when(col == 0)(lambda: load(7, vz))
        pl.when(col != 0)(lambda: load(7))
        pl.when(col == ring_len - 1)(lambda: load(8, vz))
        pl.when(col != ring_len - 1)(lambda: load(8))
        dk_acc[pl.ds(0, own), :] = jnp.zeros((own, TILE), jnp.float32)
        dv_acc[pl.ds(0, own), :] = jnp.zeros((own, TILE), jnp.float32)
        for i, (src, dst) in enumerate(moves):
            pltpu.make_async_copy(src, dst, sems.at[i]).wait()
        rows = lax.broadcasted_iota(jnp.int32, (TILE, TILE), 0)

        def span(t):
            return pl.ds(pl.multiple_of(t * TILE, TILE), TILE)

        def scores(t, p_ref):
            tile = first_tile + t
            q_t = q[span(t), :]
            top = None
            for n in range(nbr_count):
                near = nbr[tile * nbr_count + n]
                key = k_ext[span(near - ext_base), :]
                score = dot(key, q_t, NT) * scale_two
                score = jnp.where(rows < cnt[near], score, -jnp.inf)
                p_ref[n] = score
                peak = jnp.max(score, axis=0, keepdims=True)
                top = peak if top is None else jnp.maximum(top, peak)
            total = jnp.zeros((1, TILE), jnp.float32)
            for n in range(nbr_count):
                prob = jnp.exp2(p_ref[n] - top)
                p_ref[n] = prob
                total = total + jnp.sum(prob, axis=0, keepdims=True)
            stats[pl.ds(t, 1), :] = top + jnp.log2(total)
            stats[pl.ds(2 * tiles_dev + t, 1), :] = 1.0 / total

        def grads(t, p_ref):
            tile = first_tile + t
            at = span(t)
            q_t = q[at, :]
            g_t = jnp.where(rows < cnt[tile], g[at, :].astype(jnp.float32), 0.0)
            delta = jnp.sum((g_t * o[at, :].astype(jnp.float32)).T, axis=0, keepdims=True)
            stats[pl.ds(tiles_dev + t, 1), :] = delta
            inv = stats[pl.ds(2 * tiles_dev + t, 1), :]
            g_t = g_t.astype(jnp.bfloat16)
            dq = None
            for n in range(nbr_count):
                place = nbr[tile * nbr_count + n] - ext_base
                mine = place - half_tiles
                mine = jnp.where((mine >= 0) & (mine < tiles_dev), mine, tiles_dev)
                prob = p_ref[n] * inv
                dprob = dot(v_ext[span(place), :], g_t, NT)
                dscore = (prob * (dprob - delta) * scale).astype(jnp.bfloat16)
                term = dot(dscore, k_ext[span(place), :], TN)
                dq = term if dq is None else dq + term
                dk_acc[span(mine), :] += dot(dscore, q_t, NN)
                dv_acc[span(mine), :] += dot(prob.astype(jnp.bfloat16), g_t, NN)
            dq_ref[at, :] = dq.astype(jnp.bfloat16)

        scores(0, p_even)

        def step(i, carry):
            t = 2 * i
            scores(t + 1, p_odd)
            grads(t, p_even)
            scores(jnp.minimum(t + 2, tiles_dev - 1), p_even)
            grads(t + 1, p_odd)
            return carry

        lax.fori_loop(0, tiles_dev // 2, step, 0)
        dk_ref[...] = dk_acc[pl.ds(0, own), :]
        dv_ref[...] = dv_acc[pl.ds(0, own), :]
        stat_lo[pl.ds(0, half_tiles), :] = stats[pl.ds(0, half_tiles), :]
        stat_lo[pl.ds(half_tiles, half_tiles), :] = stats[pl.ds(tiles_dev, half_tiles), :]
        stat_hi[pl.ds(0, half_tiles), :] = stats[pl.ds(half_tiles, half_tiles), :]
        stat_hi[pl.ds(half_tiles, half_tiles), :] = stats[
            pl.ds(tiles_dev + half_tiles, half_tiles), :
        ]

    return kernel


def near_kernel(tiles_dev, tiles_all, nbr_count, ring_len, peers):
    half_tiles = tiles_dev // 2
    half = half_tiles * TILE
    own = tiles_dev * TILE
    share = own // peers
    scale = TILE ** (-0.5)
    scale_two = scale * math.log2(math.e)

    def kernel(
        shard, nbr, cnt, k_any, v_any, dk_any, dv_any, slo, shi, glo, ghi, qlo, qhi, qz,
        joint, k, v, dk_acc, dv_acc, q, g, stats, pairs, sems,
    ):
        s = shard[0]
        first_tile = s * tiles_dev
        col = lax.rem(s, ring_len)
        q_low = q.at[pl.ds(0, half)]
        q_high = q.at[pl.ds(half, half)]
        moves = [
            (k_any, k),
            (v_any, v),
            (dk_any, dk_acc.at[pl.ds(0, own)]),
            (dv_any, dv_acc.at[pl.ds(0, own)]),
            (slo, stats.at[0]),
            (shi, stats.at[1]),
            (glo, g.at[pl.ds(0, half)]),
            (ghi, g.at[pl.ds(half, half)]),
            (qlo, q_low),
            (qhi, q_high),
        ]

        def load(i, src=None):
            source = moves[i][0] if src is None else src
            pltpu.make_async_copy(source, moves[i][1], sems.at[i]).start()

        for i in range(8):
            load(i)
        pl.when(col == 0)(lambda: load(8, qz))
        pl.when(col != 0)(lambda: load(8))
        pl.when(col == ring_len - 1)(lambda: load(9, qz))
        pl.when(col != ring_len - 1)(lambda: load(9))

        def scan(i, count):
            tile = jnp.where(
                i < half_tiles, first_tile - half_tiles + i, first_tile + tiles_dev + i - half_tiles
            )
            inside = (tile >= 0) & (tile < tiles_all)
            safe = jnp.where(inside, tile, 0)
            for n in range(1, nbr_count):
                mine = nbr[safe * nbr_count + n] - first_tile
                hit = inside & (mine >= 0) & (mine < tiles_dev)
                pairs[0, count] = i
                pairs[1, count] = mine
                count = count + hit.astype(jnp.int32)
            return count

        count = lax.fori_loop(0, tiles_dev, scan, jnp.int32(0))
        pairs[0, count] = 0
        pairs[1, count] = tiles_dev
        for i, (src, dst) in enumerate(moves):
            pltpu.make_async_copy(src, dst, sems.at[i]).wait()
        rows = lax.broadcasted_iota(jnp.int32, (TILE, TILE), 0)

        def span(t):
            return pl.ds(pl.multiple_of(t * TILE, TILE), TILE)

        def terms(index):
            i = pairs[0, index]
            mine = pairs[1, index]
            read = jnp.minimum(mine, tiles_dev - 1)
            side = jnp.where(i < half_tiles, 0, 1)
            line = i - side * half_tiles
            tile = first_tile + jnp.where(side == 0, i - half_tiles, tiles_dev + line)
            q_t = q[span(i), :]
            held = cnt[jnp.clip(tile, 0, tiles_all - 1)]
            g_t = jnp.where(rows < held, g[span(i), :].astype(jnp.float32), 0.0)
            g_t = g_t.astype(jnp.bfloat16)
            log_row = stats[side, pl.ds(line, 1), :]
            delta = stats[side, pl.ds(half_tiles + line, 1), :]
            score = dot(k[span(read), :], q_t, NT) * scale_two
            score = jnp.where(rows < cnt[first_tile + read], score - log_row, -jnp.inf)
            prob = jnp.exp2(score)
            dprob = dot(v[span(read), :], g_t, NT)
            dscore = (prob * (dprob - delta) * scale).astype(jnp.bfloat16)
            return mine, dot(dscore, q_t, NN), dot(prob.astype(jnp.bfloat16), g_t, NN)

        def step(j, carry):
            first = terms(2 * j)
            second = terms(2 * j + 1)
            for mine, dk, dv in (first, second):
                dk_acc[span(mine), :] += dk
                dv_acc[span(mine), :] += dv
            return carry

        lax.fori_loop(0, (count + 1) // 2, step, 0)
        for which, acc in ((0, dk_acc), (1, dv_acc)):
            joint[:, which] = (
                acc[pl.ds(0, own), :].astype(jnp.bfloat16).reshape(peers, share, TILE)
            )

    return kernel


def routes(seq_count, ring_len):
    rings = seq_count // ring_len
    forward = [(i, i + 1) for i in range(seq_count - 1)]
    around = [
        (r * ring_len + x, r * ring_len + (x + 1) % ring_len)
        for r in range(rings)
        for x in range(ring_len)
    ]
    across = [(r * ring_len, (r + 1) * ring_len) for r in range(rings - 1)] + [
        ((r + 1) * ring_len - 1, r * ring_len - 1) for r in range(1, rings)
    ]
    return forward, around, across


def device_work(query_rows, key_rows, value_rows, attn_output, out_grad, neighbours, counts):
    seq_rows, batch, width = out_grad.shape
    shard_tokens, _, head_dim = query_rows.shape
    nbr_count = neighbours.shape[1]
    tiles_all = counts.shape[0]
    tiles_dev = shard_tokens // TILE
    half = shard_tokens // 2
    peers = shard_tokens // seq_rows
    seq_count = lax.axis_size("seq")
    ring_len = 4 if seq_count % 4 == 0 else seq_count
    forward, around, across = routes(seq_count, ring_len)
    backward = [(b, a) for a, b in forward]
    around_back = [(b, a) for a, b in around]
    shard = lax.axis_index("seq").astype(jnp.int32)
    at_start = lax.rem(shard, ring_len) == 0

    def ring(rows):
        return (
            lax.ppermute(rows[half:], "seq", around),
            lax.ppermute(rows[:half], "seq", around_back),
        )

    def cross(low, high):
        return lax.ppermute(jnp.where(at_start, low, high), "seq", across)

    def direct(low, high):
        return lax.ppermute(high, "seq", forward), lax.ppermute(low, "seq", backward)

    q = query_rows.reshape(shard_tokens, head_dim)
    k = key_rows.reshape(shard_tokens, head_dim)
    v = value_rows.reshape(shard_tokens, head_dim)
    o = attn_output.reshape(shard_tokens, head_dim)
    table = neighbours.reshape(-1)
    v_low, v_high = ring(v)
    k_low, k_high = direct(k[:half], k[half:])
    v_far = cross(v_low, v_high)
    sent = out_grad.reshape(seq_rows, peers, head_dim).transpose(1, 0, 2)
    grads = lax.all_to_all(sent, "head", split_axis=0, concat_axis=0, tiled=True)
    grads = grads.reshape(shard_tokens, head_dim)
    q_late, v_low, v_high = lax.optimization_barrier((q, v_low, v_high))
    q_low, q_high = ring(q_late)
    g_low, g_high = direct(grads[:half], grads[half:])
    q_low, q_high, v_far = lax.optimization_barrier((q_low, q_high, v_far))
    q_far = cross(q_low, q_high)

    smem = pl.BlockSpec(memory_space=pltpu.SMEM)
    vmem = pl.BlockSpec(memory_space=pltpu.VMEM)
    hbm = pl.BlockSpec(memory_space=pl.ANY)
    rows = jax.ShapeDtypeStruct((shard_tokens, head_dim), jnp.bfloat16)
    sums = jax.ShapeDtypeStruct((shard_tokens, head_dim), jnp.float32)
    stat = jax.ShapeDtypeStruct((tiles_dev, head_dim), jnp.float32)
    held = pltpu.VMEM((shard_tokens, head_dim), jnp.bfloat16)
    wide = pltpu.VMEM((2 * shard_tokens, head_dim), jnp.bfloat16)
    acc = pltpu.VMEM((shard_tokens + TILE, head_dim), jnp.float32)
    tile_probs = pltpu.VMEM((nbr_count, TILE, TILE), jnp.float32)
    dq, dk, dv, stat_low, stat_high = pl.pallas_call(
        own_kernel(tiles_dev, nbr_count, ring_len),
        out_shape=(rows, sums, sums, stat, stat),
        in_specs=[smem] * 3 + [hbm] * 10,
        out_specs=(vmem,) * 5,
        scratch_shapes=[
            held, held, held, wide, wide, acc, acc,
            pltpu.VMEM((3 * tiles_dev, head_dim), jnp.float32),
            tile_probs, tile_probs,
            pltpu.SemaphoreType.DMA((9,)),
        ],
        name="own",
    )(shard.reshape(1), table, counts, q, k, v, o, grads, k_low, k_high, v_low, v_high, v_far)
    stat_low, stat_high = direct(stat_low, stat_high)
    back_q = lax.all_to_all(
        dq.reshape(peers, seq_rows, head_dim), "head", split_axis=0, concat_axis=0, tiled=True
    )
    joint = pl.pallas_call(
        near_kernel(tiles_dev, tiles_all, nbr_count, ring_len, peers),
        out_shape=jax.ShapeDtypeStruct((peers, 2, seq_rows, head_dim), jnp.bfloat16),
        in_specs=[smem] * 3 + [hbm] * 11,
        out_specs=vmem,
        scratch_shapes=[
            held, held, acc, acc, held, held,
            pltpu.VMEM((2, tiles_dev, head_dim), jnp.float32),
            pltpu.SMEM((2, tiles_dev * nbr_count), jnp.int32),
            pltpu.SemaphoreType.DMA((10,)),
        ],
        name="near",
    )(
        shard.reshape(1), table, counts, k, v, dk, dv,
        stat_low, stat_high, g_low, g_high, q_low, q_high, q_far,
    )
    back_kv = lax.all_to_all(joint, "head", split_axis=0, concat_axis=0, tiled=True)

    def to_rows(block):
        return block.transpose(1, 0, 2).reshape(seq_rows, batch, width)

    return to_rows(back_q), to_rows(back_kv[:, 0]), to_rows(back_kv[:, 1])


def solution(mesh):
    placed = (
        P("seq", "head", None),
        P("seq", "head", None),
        P("seq", "head", None),
        P("seq", "head", None),
        P(("seq", "head"), None, None),
        P(),
        P(),
    )
    return jax.shard_map(
        device_work,
        mesh=mesh,
        in_specs=placed,
        out_specs=(
            P(("seq", "head"), None, None),
            P(("seq", "head"), None, None),
            P(("seq", "head"), None, None),
        ),
        check_vma=False,
    )
```

time: 193 us -> 197 us (1.021)
  the two profiles are of different devices: /device:TPU:1 before, /device:TPU:7 now
where the time goes in v2:
time: 197 us; the launch traced here: 196 us
  waiting for transfers between devices  81.9 us (42%)
  starting transfers between devices  80.7 us (41%)
  Pallas kernels  24.1 us (12%)
  local copies, waits for them, and re-layouts  8.6 us (4%)
    ppermute x3, starting transfers between devices, direct(): lax.ppermute(high, 'seq', forward)  28.6 us
    ppermute x3, waiting for transfers between devices, direct(): lax.ppermute(low, 'seq', backward)  28.1 us
    all_to_all x1, waiting for transfers between devices, device_work(): lax.all_to_all(joint, 'head', split_axis=0, concat_axis=0, tiled=True)  27.5 us
    ppermute x2, waiting for transfers between devices, cross(): return lax.ppermute(jnp.where(at_start, low, high), 'seq', across)  19.4 us
    pallas_call x1, Pallas kernels, device_work(): pl.pallas_call(own_kernel(tiles_dev, nbr_count, ring_len), out_shape=(row...  17.6 us
    all_to_all x1, starting transfers between devices, device_work(): lax.all_to_all(sent, 'head', split_axis=0, concat_axis=0, tiled=True)  13.9 us
    all_to_all x1, starting transfers between devices, device_work(): lax.all_to_all(dq.reshape(peers, seq_rows, head_dim), 'head', split_axis=...  10 us
    all_to_all x1, starting transfers between devices, device_work(): lax.all_to_all(joint, 'head', split_axis=0, concat_axis=0, tiled=True)  8.96 us
  transfers between devices with their start and end apart: 15, of which 7 were waited for; matrix products, arithmetic and copies ran while one was open for 1% of the time, Pallas kernels for 3%

profile of v2, /device:TPU:7, one launch (start us, length us, event | category | flops | bytes accessed | tf_op | source)
XLA Modules:
  0.0 196.4 jit_solution(672839051845898403)
XLA Ops:
  0.6 1.4 reshape.55
  3.1 13.9 %all-to-all-start = ((bf16[64,32,128]{2,1,0:T(8,128)(2,1)}), bf16[64,32,128]{2,1,0:T(8,128)(2,1)S(1)}, u32[]{:S(2)}, u32[]{:S(2)}) async-start(bf16[64,32,128]{2,1,0:T(8,128)(2,1)} %bitcast.28), calls=%async_computation | async-start | bytes 1048576 | tf_op jit(solution)/shard_map/all_to_all | solution.py:288
  17.1 2.2 %collective-permute-start.2 = (bf16[1024,128]{1,0:T(8,128)(2,1)S(1)}, bf16[1024,128]{1,0:T(8,128)(2,1)S(1)}, u32[]{:S(2)}, u32[]{:S(2)}) collective-permute-start(bf16[1024,128]{1,0:T(8,128)(2,1)S(1)} %get-tuple-element.32), channel_id=1, source_target_pairs={{0,64},{64,128},{128,192},{192,0},{256,320},{320,384},{384,448},{4... | collective-permute-start | bytes 786440 | tf_op jit(solution)/shard_map/ppermute | solution.py:269
  19.4 3.2 %collective-permute-start.3 = (bf16[1024,128]{1,0:T(8,128)(2,1)S(1)}, bf16[1024,128]{1,0:T(8,128)(2,1)S(1)}, u32[]{:S(2)}, u32[]{:S(2)}) collective-permute-start(bf16[1024,128]{1,0:T(8,128)(2,1)S(1)} %get-tuple-element.31), channel_id=1, source_target_pairs={{64,0},{128,64},{192,128},{0,192},{320,256},{384,320},{448,384},{2... | collective-permute-start | bytes 786440 | tf_op jit(solution)/shard_map/ppermute | solution.py:270
  22.6 3.9 %collective-permute-done.2.vlo = bf16[1024,128]{1,0:T(8,128)(2,1)S(1)} collective-permute-done((bf16[1024,128]{1,0:T(8,128)(2,1)S(1)}, bf16[1024,128]{1,0:T(8,128)(2,1)S(1)}, u32[]{:S(2)}, u32[]{:S(2)}) %collective-permute-start.2) | collective-permute-done | bytes 262176 | tf_op jit(solution)/shard_map/ppermute | solution.py:269
  26.5 3.0 %collective-permute-done.3.vhi = bf16[1024,128]{1,0:T(8,128)(2,1)S(1)} collective-permute-done((bf16[1024,128]{1,0:T(8,128)(2,1)S(1)}, bf16[1024,128]{1,0:T(8,128)(2,1)S(1)}, u32[]{:S(2)}, u32[]{:S(2)}) %collective-permute-start.3) | collective-permute-done | bytes 262176 | tf_op jit(solution)/shard_map/ppermute | solution.py:270
  29.6 2.0 %collective-permute-start.4 = (bf16[1024,128]{1,0:T(8,128)(2,1)S(1)}, bf16[1024,128]{1,0:T(8,128)(2,1)S(1)}, u32[]{:S(2)}, u32[]{:S(2)}) collective-permute-start(bf16[1024,128]{1,0:T(8,128)(2,1)S(1)} %get-tuple-element.30), channel_id=1, source_target_pairs={{0,64},{64,128},{128,192},{192,0},{256,320},{320,384},{384,448},{4... | collective-permute-start | bytes 786440 | tf_op jit(solution)/shard_map/ppermute | solution.py:269
  31.6 3.3 %collective-permute-start.5 = (bf16[1024,128]{1,0:T(8,128)(2,1)S(1)}, bf16[1024,128]{1,0:T(8,128)(2,1)S(1)}, u32[]{:S(2)}, u32[]{:S(2)}) collective-permute-start(bf16[1024,128]{1,0:T(8,128)(2,1)S(1)} %get-tuple-element.29), channel_id=1, source_target_pairs={{64,0},{128,64},{192,128},{0,192},{320,256},{384,320},{448,384},{2... | collective-permute-start | bytes 786440 | tf_op jit(solution)/shard_map/ppermute | solution.py:270
  36.2 15.9 %collective-permute-start = (bf16[1024,128]{1,0:T(8,128)(2,1)S(1)}, bf16[1024,128]{1,0:T(8,128)(2,1)S(1)}, u32[]{:S(2)}, u32[]{:S(2)}) collective-permute-start(bf16[1024,128]{1,0:T(8,128)(2,1)S(1)} %get-tuple-element.34), channel_id=1, source_target_pairs={{0,64},{64,128},{128,192},{192,256},{256,320},{320,384},{384,448},... | collective-permute-start | bytes 786440 | tf_op jit(solution)/shard_map/ppermute | solution.py:277
  52.1 1.9 collective-permute-start.1
  54.9 12.9 %collective-permute-done.6.vz = bf16[1024,128]{1,0:T(8,128)(2,1)S(1)} collective-permute-done((bf16[1024,128]{1,0:T(8,128)(2,1)S(1)}, bf16[1024,128]{1,0:T(8,128)(2,1)S(1)}, u32[]{:S(2)}, u32[]{:S(2)}) %collective-permute-start.6) | collective-permute-done | bytes 262176 | tf_op jit(solution)/shard_map/ppermute | solution.py:274
  67.8 15.3 %collective-permute-done.1.khi = bf16[1024,128]{1,0:T(8,128)(2,1)S(1)} collective-permute-done((bf16[1024,128]{1,0:T(8,128)(2,1)S(1)}, bf16[1024,128]{1,0:T(8,128)(2,1)S(1)}, u32[]{:S(2)}, u32[]{:S(2)}) %collective-permute-start.1) | collective-permute-done | bytes 262176 | tf_op jit(solution)/shard_map/ppermute | solution.py:277
  84.0 17.6 %own.1 = (bf16[2048,128]{1,0:T(8,128)(2,1)}, f32[2048,128]{1,0:T(8,128)}, f32[2048,128]{1,0:T(8,128)}, f32[16,128]{1,0:T(8,128)}, f32[16,128]{1,0:T(8,128)}) custom-call(s32[1]{0:T(128)} %bitcast.shard, s32[768]{0:T(1024)} %reshape.50.nbr, s32[192]{0:T(256)} %cnt.3, bf16[2048,128]{1,0:T(8,128)(2,1)} %bitcast.34, bf16[2048,128]{1,0:T(8,128)(2,1)} %bitcast.30, ...), custom_call_target="tpu_custom_call" | custom-call | tf_op jit(solution)/shard_map/own/pallas_call | solution.py:306
  101.6 10.0 %all-to-all-start.1 = ((bf16[64,32,128]{2,1,0:T(8,128)(2,1)}), bf16[64,32,128]{2,1,0:T(8,128)(2,1)S(1)}, u32[]{:S(2)}, u32[]{:S(2)}) async-start(bf16[64,32,128]{2,1,0:T(8,128)(2,1)} %bitcast.38), calls=%async_computation.1 | async-start | bytes 1048576 | tf_op jit(solution)/shard_map/all_to_all | solution.py:320
  111.7 1.4 collective-permute-start.11
  113.2 3.3 %collective-permute-start.9 = (bf16[1024,128]{1,0:T(8,128)(2,1)S(1)}, bf16[1024,128]{1,0:T(8,128)(2,1)S(1)}, u32[]{:S(2)}, u32[]{:S(2)}) collective-permute-start(bf16[1024,128]{1,0:T(8,128)(2,1)S(1)} %bitcast.40), channel_id=1, source_target_pairs={{0,64},{64,128},{128,192},{192,256},{256,320},{320,384},{384,448},... | collective-permute-start | bytes 786440 | tf_op jit(solution)/shard_map/ppermute | solution.py:277
  116.6 2.0 collective-permute-start.10
  118.6 9.3 %collective-permute-start.7 = (f32[16,128]{1,0:T(8,128)S(1)}, f32[16,128]{1,0:T(8,128)S(1)}, u32[]{:S(2)}, u32[]{:S(2)}) collective-permute-start(f32[16,128]{1,0:T(8,128)S(1)} %copy-done.19), channel_id=1, source_target_pairs={{0,64},{64,128},{128,192},{192,256},{256,320},{320,384},{384,448},... | collective-permute-start | bytes 24584 | tf_op jit(solution)/shard_map/ppermute | solution.py:277
  127.9 1.9 collective-permute-start.8
  129.8 6.5 %collective-permute-done.11.qz = bf16[1024,128]{1,0:T(8,128)(2,1)S(1)} collective-permute-done((bf16[1024,128]{1,0:T(8,128)(2,1)S(1)}, bf16[1024,128]{1,0:T(8,128)(2,1)S(1)}, u32[]{:S(2)}, u32[]{:S(2)}) %collective-permute-start.11) | collective-permute-done | bytes 262176 | tf_op jit(solution)/shard_map/ppermute | solution.py:274
  136.4 12.8 %collective-permute-done.8.shi = f32[16,128]{1,0:T(8,128)S(1)} collective-permute-done((f32[16,128]{1,0:T(8,128)S(1)}, f32[16,128]{1,0:T(8,128)S(1)}, u32[]{:S(2)}, u32[]{:S(2)}) %collective-permute-start.8) | collective-permute-done | bytes 8224 | tf_op jit(solution)/shard_map/ppermute | solution.py:277
  150.0 6.5 %near.1 = bf16[64,2,32,128]{3,2,1,0:T(8,128)(2,1)} custom-call(s32[1]{0:T(128)} %bitcast.shard, s32[768]{0:T(1024)} %reshape.50.nbr, s32[192]{0:T(256)} %cnt.3, bf16[2048,128]{1,0:T(8,128)(2,1)} %bitcast.31, bf16[2048,128]{1,0:T(8,128)(2,1)} %bitcast.33, f32[2048,128]{1,0:T(8,128)} %get-tuple-element.19.dk_any, f32[2048,128]{1,0:T(8,128)} %get-tuple-element.20.dv_any, ...), custom_call_target="tpu_custom_call" | custom-call | tf_op jit(solution)/shard_map/near/pallas_call | solution.py:323
  156.5 9.0 %all-to-all-start.2 = ((bf16[64,2,32,128]{3,2,1,0:T(8,128)(2,1)}), bf16[64,2,32,128]{3,2,1,0:T(8,128)(2,1)S(1)}, u32[]{:S(2)}, u32[]{:S(2)}) async-start(bf16[64,2,32,128]{3,2,1,0:T(8,128)(2,1)} %near.1), calls=%async_computation.2 | async-start | bytes 2097152 | tf_op jit(solution)/shard_map/all_to_all | solution.py:339
  166.6 27.5 %all-to-all-done.2 = bf16[64,2,32,128]{3,2,1,0:T(8,128)(2,1)S(1)} async-done(((bf16[64,2,32,128]{3,2,1,0:T(8,128)(2,1)}), bf16[64,2,32,128]{3,2,1,0:T(8,128)(2,1)S(1)}, u32[]{:S(2)}, u32[]{:S(2)}) %all-to-all-start.2) | async-done | bytes 1048608 | tf_op jit(solution)/shard_map/all_to_all | solution.py:339
  (65 shorter events, 8.6 us)
Async XLA Ops:
  3.1 13.9 %copy-start.3 = (bf16[2048,1,128]{2,0,1:T(8,128)(2,1)S(1)}, bf16[2048,1,128]{2,0,1:T(8,128)(2,1)}, u32[]{:S(2)}) copy-start(bf16[2048,1,128]{2,0,1:T(8,128)(2,1)} %param.9) | copy-start | bytes 1572868
  3.1 80.0 %all-to-all-start = ((bf16[64,32,128]{2,1,0:T(8,128)(2,1)}), bf16[64,32,128]{2,1,0:T(8,128)(2,1)S(1)}, u32[]{:S(2)}, u32[]{:S(2)}) async-start(bf16[64,32,128]{2,1,0:T(8,128)(2,1)} %bitcast.28), calls=%async_computation | async-start | bytes 1048576 | tf_op jit(solution)/shard_map/all_to_all | solution.py:288
  17.1 9.4 %collective-permute-start.2 = (bf16[1024,128]{1,0:T(8,128)(2,1)S(1)}, bf16[1024,128]{1,0:T(8,128)(2,1)S(1)}, u32[]{:S(2)}, u32[]{:S(2)}) collective-permute-start(bf16[1024,128]{1,0:T(8,128)(2,1)S(1)} %get-tuple-element.32), channel_id=1, source_target_pairs={{0,64},{64,128},{128,192},{192,0},{256,320},{320,384},{384,448},{4... | collective-permute-start | bytes 786440 | tf_op jit(solution)/shard_map/ppermute | solution.py:269
  19.4 10.2 %collective-permute-start.3 = (bf16[1024,128]{1,0:T(8,128)(2,1)S(1)}, bf16[1024,128]{1,0:T(8,128)(2,1)S(1)}, u32[]{:S(2)}, u32[]{:S(2)}) collective-permute-start(bf16[1024,128]{1,0:T(8,128)(2,1)S(1)} %get-tuple-element.31), channel_id=1, source_target_pairs={{64,0},{128,64},{192,128},{0,192},{320,256},{384,320},{448,384},{2... | collective-permute-start | bytes 786440 | tf_op jit(solution)/shard_map/ppermute | solution.py:270
  29.6 25.4 %collective-permute-start.4 = (bf16[1024,128]{1,0:T(8,128)(2,1)S(1)}, bf16[1024,128]{1,0:T(8,128)(2,1)S(1)}, u32[]{:S(2)}, u32[]{:S(2)}) collective-permute-start(bf16[1024,128]{1,0:T(8,128)(2,1)S(1)} %get-tuple-element.30), channel_id=1, source_target_pairs={{0,64},{64,128},{128,192},{192,0},{256,320},{320,384},{384,448},{4... | collective-permute-start | bytes 786440 | tf_op jit(solution)/shard_map/ppermute | solution.py:269
  31.6 23.4 %collective-permute-start.5 = (bf16[1024,128]{1,0:T(8,128)(2,1)S(1)}, bf16[1024,128]{1,0:T(8,128)(2,1)S(1)}, u32[]{:S(2)}, u32[]{:S(2)}) collective-permute-start(bf16[1024,128]{1,0:T(8,128)(2,1)S(1)} %get-tuple-element.29), channel_id=1, source_target_pairs={{64,0},{128,64},{192,128},{0,192},{320,256},{384,320},{448,384},{2... | collective-permute-start | bytes 786440 | tf_op jit(solution)/shard_map/ppermute | solution.py:270
  34.9 19.2 %copy-start.17 = (s32[192,4]{0,1:T(4,128)S(1)}, s32[192,4]{0,1:T(4,128)}, u32[]{:S(2)}) copy-start(s32[192,4]{0,1:T(4,128)} %param.12) | copy-start | bytes 9220
  34.9 32.9 %collective-permute-start.6 = (bf16[1024,128]{1,0:T(8,128)(2,1)S(1)}, bf16[1024,128]{1,0:T(8,128)(2,1)S(1)}, u32[]{:S(2)}, u32[]{:S(2)}) collective-permute-start(bf16[1024,128]{1,0:T(8,128)(2,1)S(1)} %broadcast_select_fusion.1), channel_id=1, source_target_pairs={{0,256},{256,512},{448,192},{704,448},{1,257},{257,513},{449,193},... | collective-permute-start | bytes 786440 | tf_op jit(solution)/shard_map/ppermute | solution.py:274
  36.2 31.6 %collective-permute-start = (bf16[1024,128]{1,0:T(8,128)(2,1)S(1)}, bf16[1024,128]{1,0:T(8,128)(2,1)S(1)}, u32[]{:S(2)}, u32[]{:S(2)}) collective-permute-start(bf16[1024,128]{1,0:T(8,128)(2,1)S(1)} %get-tuple-element.34), channel_id=1, source_target_pairs={{0,64},{64,128},{128,192},{192,256},{256,320},{320,384},{384,448},... | collective-permute-start | bytes 786440 | tf_op jit(solution)/shard_map/ppermute | solution.py:277
  52.1 31.0 %collective-permute-start.1 = (bf16[1024,128]{1,0:T(8,128)(2,1)S(1)}, bf16[1024,128]{1,0:T(8,128)(2,1)S(1)}, u32[]{:S(2)}, u32[]{:S(2)}) collective-permute-start(bf16[1024,128]{1,0:T(8,128)(2,1)S(1)} %get-tuple-element.33), channel_id=1, source_target_pairs={{64,0},{128,64},{192,128},{256,192},{320,256},{384,320},{448,384},... | collective-permute-start | bytes 786440 | tf_op jit(solution)/shard_map/ppermute | solution.py:277
  54.9 56.8 %copy-start.5 = (bf16[1024,128]{1,0:T(8,128)(2,1)}, bf16[1024,128]{1,0:T(8,128)(2,1)S(1)}, u32[]{:S(2)}) copy-start(bf16[1024,128]{1,0:T(8,128)(2,1)S(1)} %collective-permute-done.4.qlo) | copy-start | bytes 786436
  54.9 56.8 %copy-start.6 = (bf16[1024,128]{1,0:T(8,128)(2,1)}, bf16[1024,128]{1,0:T(8,128)(2,1)S(1)}, u32[]{:S(2)}) copy-start(bf16[1024,128]{1,0:T(8,128)(2,1)S(1)} %collective-permute-done.5.qhi) | copy-start | bytes 786436
  67.8 15.3 %copy-start.12 = (bf16[1024,128]{1,0:T(8,128)(2,1)}, bf16[1024,128]{1,0:T(8,128)(2,1)S(1)}, u32[]{:S(2)}) copy-start(bf16[1024,128]{1,0:T(8,128)(2,1)S(1)} %collective-permute-done.6.vz) | copy-start | bytes 786436
  67.8 15.3 %copy-start.13 = (bf16[1024,128]{1,0:T(8,128)(2,1)}, bf16[1024,128]{1,0:T(8,128)(2,1)S(1)}, u32[]{:S(2)}) copy-start(bf16[1024,128]{1,0:T(8,128)(2,1)S(1)} %collective-permute-done.klo) | copy-start | bytes 786436
  101.6 54.8 %all-to-all-start.1 = ((bf16[64,32,128]{2,1,0:T(8,128)(2,1)}), bf16[64,32,128]{2,1,0:T(8,128)(2,1)S(1)}, u32[]{:S(2)}, u32[]{:S(2)}) async-start(bf16[64,32,128]{2,1,0:T(8,128)(2,1)} %bitcast.38), calls=%async_computation.1 | async-start | bytes 1048576 | tf_op jit(solution)/shard_map/all_to_all | solution.py:320
  111.7 24.6 %collective-permute-start.11 = (bf16[1024,128]{1,0:T(8,128)(2,1)S(1)}, bf16[1024,128]{1,0:T(8,128)(2,1)S(1)}, u32[]{:S(2)}, u32[]{:S(2)}) collective-permute-start(bf16[1024,128]{1,0:T(8,128)(2,1)S(1)} %broadcast_select_fusion), channel_id=1, source_target_pairs={{0,256},{256,512},{448,192},{704,448},{1,257},{257,513},{449,193},... | collective-permute-start | bytes 786440 | tf_op jit(solution)/shard_map/ppermute | solution.py:274
  113.2 14.7 %copy-start.18 = (f32[16,128]{1,0:T(8,128)S(1)}, f32[16,128]{1,0:T(8,128)}, u32[]{:S(2)}) copy-start(f32[16,128]{1,0:T(8,128)} %get-tuple-element.22) | copy-start | bytes 24580
  113.2 36.0 %collective-permute-start.9 = (bf16[1024,128]{1,0:T(8,128)(2,1)S(1)}, bf16[1024,128]{1,0:T(8,128)(2,1)S(1)}, u32[]{:S(2)}, u32[]{:S(2)}) collective-permute-start(bf16[1024,128]{1,0:T(8,128)(2,1)S(1)} %bitcast.40), channel_id=1, source_target_pairs={{0,64},{64,128},{128,192},{192,256},{256,320},{320,384},{384,448},... | collective-permute-start | bytes 786440 | tf_op jit(solution)/shard_map/ppermute | solution.py:277
  116.6 32.6 %collective-permute-start.10 = (bf16[1024,128]{1,0:T(8,128)(2,1)S(1)}, bf16[1024,128]{1,0:T(8,128)(2,1)S(1)}, u32[]{:S(2)}, u32[]{:S(2)}) collective-permute-start(bf16[1024,128]{1,0:T(8,128)(2,1)S(1)} %bitcast.39), channel_id=1, source_target_pairs={{64,0},{128,64},{192,128},{256,192},{320,256},{384,320},{448,384},... | collective-permute-start | bytes 786440 | tf_op jit(solution)/shard_map/ppermute | solution.py:277
  118.6 17.8 %collective-permute-start.7 = (f32[16,128]{1,0:T(8,128)S(1)}, f32[16,128]{1,0:T(8,128)S(1)}, u32[]{:S(2)}, u32[]{:S(2)}) collective-permute-start(f32[16,128]{1,0:T(8,128)S(1)} %copy-done.19), channel_id=1, source_target_pairs={{0,64},{64,128},{128,192},{192,256},{256,320},{320,384},{384,448},... | collective-permute-start | bytes 24584 | tf_op jit(solution)/shard_map/ppermute | solution.py:277
  127.9 21.3 %collective-permute-start.8 = (f32[16,128]{1,0:T(8,128)S(1)}, f32[16,128]{1,0:T(8,128)S(1)}, u32[]{:S(2)}, u32[]{:S(2)}) collective-permute-start(f32[16,128]{1,0:T(8,128)S(1)} %copy-done.18), channel_id=1, source_target_pairs={{64,0},{128,64},{192,128},{256,192},{320,256},{384,320},{448,384},... | collective-permute-start | bytes 24584 | tf_op jit(solution)/shard_map/ppermute | solution.py:277
  136.4 12.9 %copy-start.9 = (bf16[1024,128]{1,0:T(8,128)(2,1)}, bf16[1024,128]{1,0:T(8,128)(2,1)S(1)}, u32[]{:S(2)}) copy-start(bf16[1024,128]{1,0:T(8,128)(2,1)S(1)} %collective-permute-done.11.qz) | copy-start | bytes 786436
  136.4 12.9 %copy-start.15 = (f32[16,128]{1,0:T(8,128)}, f32[16,128]{1,0:T(8,128)S(1)}, u32[]{:S(2)}) copy-start(f32[16,128]{1,0:T(8,128)S(1)} %collective-permute-done.7.slo) | copy-start | bytes 24580
  156.5 37.6 %all-to-all-start.2 = ((bf16[64,2,32,128]{3,2,1,0:T(8,128)(2,1)}), bf16[64,2,32,128]{3,2,1,0:T(8,128)(2,1)S(1)}, u32[]{:S(2)}, u32[]{:S(2)}) async-start(bf16[64,2,32,128]{3,2,1,0:T(8,128)(2,1)} %near.1), calls=%async_computation.2 | async-start | bytes 2097152 | tf_op jit(solution)/shard_map/all_to_all | solution.py:339
  (11 other events, 36.6 us)

commit v3 on v2

v3 whole, which is shorter than its diff:
```python
import math

import jax
import jax.numpy as jnp
from jax import lax
from jax.experimental import pallas as pl
from jax.experimental.pallas import tpu as pltpu
from jax.sharding import PartitionSpec as P

TILE = 128
NT = (((1,), (1,)), ((), ()))
NN = (((1,), (0,)), ((), ()))
TN = (((0,), (0,)), ((), ()))


def dot(a, b, dims):
    return lax.dot_general(a, b, dims, preferred_element_type=jnp.float32)


def span(t):
    return pl.ds(pl.multiple_of(t * TILE, TILE), TILE)


def start_copies(moves, sems):
    for i, (dst, choice) in enumerate(moves):
        if len(choice) == 1:
            pltpu.make_async_copy(choice[0], dst, sems.at[i]).start()
        else:
            far, use_far, near = choice

            @pl.when(use_far)
            def _():
                pltpu.make_async_copy(far, dst, sems.at[i]).start()

            @pl.when(jnp.logical_not(use_far))
            def _():
                pltpu.make_async_copy(near, dst, sems.at[i]).start()


def wait_copies(moves, sems):
    for i, (dst, choice) in enumerate(moves):
        pltpu.make_async_copy(choice[-1], dst, sems.at[i]).wait()


def stats_kernel(tiles_dev, nbr_count, ring_len):
    half_tiles = tiles_dev // 2
    half = half_tiles * TILE
    own = tiles_dev * TILE
    scale_two = TILE ** (-0.5) * math.log2(math.e)

    def kernel(
        shard, nbr, cnt, q_any, k_any, o_any, g_any, kv_lo, kv_hi, kz,
        stat_all, stat_lo, stat_hi,
        q, o, g, k_ext, sems,
    ):
        s = shard[0]
        first_tile = s * tiles_dev
        ext_base = first_tile - half_tiles
        col = lax.rem(s, ring_len)
        moves = (
            (k_ext.at[pl.ds(half, own)], (k_any,)),
            (q, (q_any,)),
            (o, (o_any,)),
            (g, (g_any,)),
            (k_ext.at[pl.ds(0, half)], (kz, col == 0, kv_lo.at[pl.ds(0, half)])),
            (
                k_ext.at[pl.ds(half + own, half)],
                (kz, col == ring_len - 1, kv_hi.at[pl.ds(0, half)]),
            ),
        )
        start_copies(moves, sems)
        wait_copies(moves, sems)
        rows = lax.broadcasted_iota(jnp.int32, (TILE, TILE), 0)

        def lse_of(t):
            tile = first_tile + t
            q_t = q[span(t), :]
            tops, totals = [], []
            for n in range(nbr_count):
                near = nbr[tile * nbr_count + n]
                score = dot(k_ext[span(near - ext_base), :], q_t, NT) * scale_two
                score = jnp.where(rows < cnt[near], score, -jnp.inf)
                peak = jnp.max(score, axis=0, keepdims=True)
                tops.append(peak)
                totals.append(jnp.sum(jnp.exp2(score - peak), axis=0, keepdims=True))
            top = tops[0]
            for peak in tops[1:]:
                top = jnp.maximum(top, peak)
            total = totals[0] * jnp.exp2(tops[0] - top)
            for part, peak in zip(totals[1:], tops[1:]):
                total = total + part * jnp.exp2(peak - top)
            g_t = jnp.where(rows < cnt[tile], g[span(t), :].astype(jnp.float32), 0.0)
            prod = g_t * o[span(t), :].astype(jnp.float32)
            delta = jnp.sum(prod.T, axis=0, keepdims=True)
            return top + jnp.log2(total), delta

        def step(i, carry):
            first = lse_of(2 * i)
            second = lse_of(2 * i + 1)
            for t, (log_row, delta) in ((2 * i, first), (2 * i + 1, second)):
                stat_all[pl.ds(t, 1), :] = log_row
                stat_all[pl.ds(tiles_dev + t, 1), :] = delta
            return carry

        lax.fori_loop(0, tiles_dev // 2, step, 0)
        for side, out in ((0, stat_lo), (1, stat_hi)):
            out[pl.ds(0, half_tiles), :] = stat_all[pl.ds(side * half_tiles, half_tiles), :]
            out[pl.ds(half_tiles, half_tiles), :] = stat_all[
                pl.ds(tiles_dev + side * half_tiles, half_tiles), :
            ]

    return kernel


def grads_kernel(tiles_dev, tiles_all, nbr_count, ring_len, peers):
    half_tiles = tiles_dev // 2
    half = half_tiles * TILE
    own = tiles_dev * TILE
    share = own // peers
    tile_peers = TILE // share
    scale = TILE ** (-0.5)
    scale_two = scale * math.log2(math.e)

    def kernel(
        shard, nbr, cnt, q_any, k_any, v_any, g_any, kv_lo, kv_hi, kz, vz,
        qg_lo, qg_hi, qz, gz, stat_any, slo, shi,
        joint, q, g, k_ext, v_ext, q_near, g_near, dk_acc, dv_acc, stats, stats_near, pairs, sems,
    ):
        s = shard[0]
        first_tile = s * tiles_dev
        ext_base = first_tile - half_tiles
        col = lax.rem(s, ring_len)
        at_low = col == 0
        at_high = col == ring_len - 1
        first_half = pl.ds(0, half)
        second_half = pl.ds(half, half)
        above = pl.ds(half + own, half)
        moves = (
            (k_ext.at[pl.ds(half, own)], (k_any,)),
            (v_ext.at[pl.ds(half, own)], (v_any,)),
            (q, (q_any,)),
            (g, (g_any,)),
            (stats, (stat_any,)),
            (stats_near.at[0], (slo,)),
            (stats_near.at[1], (shi,)),
            (k_ext.at[first_half], (kz, at_low, kv_lo.at[first_half])),
            (k_ext.at[above], (kz, at_high, kv_hi.at[first_half])),
            (v_ext.at[first_half], (vz, at_low, kv_lo.at[second_half])),
            (v_ext.at[above], (vz, at_high, kv_hi.at[second_half])),
            (q_near.at[first_half], (qz, at_low, qg_lo.at[first_half])),
            (q_near.at[second_half], (qz, at_high, qg_hi.at[first_half])),
            (g_near.at[first_half], (gz, at_low, qg_lo.at[second_half])),
            (g_near.at[second_half], (gz, at_high, qg_hi.at[second_half])),
        )
        start_copies(moves, sems)
        zero = jnp.zeros((own, TILE), jnp.float32)
        dk_acc[pl.ds(0, own), :] = zero
        dv_acc[pl.ds(0, own), :] = zero

        def scan(i, count):
            tile = jnp.where(
                i < half_tiles, first_tile - half_tiles + i, first_tile + tiles_dev + i - half_tiles
            )
            inside = (tile >= 0) & (tile < tiles_all)
            safe = jnp.where(inside, tile, 0)
            for n in range(1, nbr_count):
                mine = nbr[safe * nbr_count + n] - first_tile
                hit = inside & (mine >= 0) & (mine < tiles_dev)
                pairs[0, count] = i
                pairs[1, count] = mine
                count = count + hit.astype(jnp.int32)
            return count

        count = lax.fori_loop(0, tiles_dev, scan, jnp.int32(0))
        pairs[0, count] = 0
        pairs[1, count] = tiles_dev
        wait_copies(moves, sems)
        rows = lax.broadcasted_iota(jnp.int32, (TILE, TILE), 0)

        def queries(ref, t, tile):
            g_t = jnp.where(rows < cnt[tile], ref[span(t), :].astype(jnp.float32), 0.0)
            return g_t.astype(jnp.bfloat16)

        def terms(place, held, q_t, g_t, log_row, delta):
            key = k_ext[span(place), :]
            score = dot(key, q_t, NT) * scale_two
            prob = jnp.exp2(jnp.where(rows < held, score - log_row, -jnp.inf))
            dprob = dot(v_ext[span(place), :], g_t, NT)
            dscore = (prob * (dprob - delta) * scale).astype(jnp.bfloat16)
            return key, prob.astype(jnp.bfloat16), dscore

        def own_step(t, carry):
            tile = first_tile + t
            q_t = q[span(t), :]
            g_t = queries(g, t, tile)
            log_row = stats[pl.ds(t, 1), :]
            delta = stats[pl.ds(tiles_dev + t, 1), :]
            places, keys, probs, dscores = [], [], [], []
            for n in range(nbr_count):
                near = nbr[tile * nbr_count + n]
                place = near - ext_base
                mine = place - half_tiles
                places.append(jnp.where((mine >= 0) & (mine < tiles_dev), mine, tiles_dev))
                key, prob, dscore = terms(place, cnt[near], q_t, g_t, log_row, delta)
                keys.append(key)
                probs.append(prob)
                dscores.append(dscore)
            dq = dot(jnp.concatenate(dscores), jnp.concatenate(keys), TN)
            sums = [(dot(ds, q_t, NN), dot(pb, g_t, NN)) for ds, pb in zip(dscores, probs)]
            for mine, (dk, dv) in zip(places, sums):
                dk_acc[span(mine), :] += dk
                dv_acc[span(mine), :] += dv
            joint[pl.ds(t * tile_peers, tile_peers), 0] = (
                dq.astype(jnp.bfloat16).reshape(tile_peers, share, TILE)
            )
            return carry

        lax.fori_loop(0, tiles_dev, own_step, 0)

        def near_terms(index):
            i = pairs[0, index]
            mine = pairs[1, index]
            read = jnp.minimum(mine, tiles_dev - 1)
            side = jnp.where(i < half_tiles, 0, 1)
            line = i - side * half_tiles
            tile = first_tile + jnp.where(side == 0, i - half_tiles, tiles_dev + line)
            q_t = q_near[span(i), :]
            g_t = queries(g_near, i, jnp.clip(tile, 0, tiles_all - 1))
            log_row = stats_near[side, pl.ds(line, 1), :]
            delta = stats_near[side, pl.ds(half_tiles + line, 1), :]
            held = cnt[first_tile + read]
            _, prob, dscore = terms(read + half_tiles, held, q_t, g_t, log_row, delta)
            return mine, dot(dscore, q_t, NN), dot(prob, g_t, NN)

        def near_step(j, carry):
            first = near_terms(2 * j)
            second = near_terms(2 * j + 1)
            for mine, dk, dv in (first, second):
                dk_acc[span(mine), :] += dk
                dv_acc[span(mine), :] += dv
            return carry

        lax.fori_loop(0, (count + 1) // 2, near_step, 0)
        for which, acc in ((1, dk_acc), (2, dv_acc)):
            joint[:, which] = (
                acc[pl.ds(0, own), :].astype(jnp.bfloat16).reshape(peers, share, TILE)
            )

    return kernel


def routes(seq_count, ring_len):
    spots = [divmod(s, ring_len) for s in range(seq_count)]

    def pairs(move):
        out = []
        for s, (r, x) in enumerate(spots):
            to = move(r, x)
            if to is not None and 0 <= to[0] < seq_count // ring_len:
                out.append((s, to[0] * ring_len + to[1]))
        return out

    last = ring_len - 1

    def ends(at_first, at_last):
        return pairs(lambda r, x: at_first(r) if x == 0 else at_last(r) if x == last else None)

    return {
        "forward": [(i, i + 1) for i in range(seq_count - 1)],
        "backward": [(i + 1, i) for i in range(seq_count - 1)],
        "around": pairs(lambda r, x: (r, (x + 1) % ring_len)),
        "around_back": pairs(lambda r, x: (r, (x - 1) % ring_len)),
        "up": pairs(lambda r, x: (r, x + 1) if x < last else None),
        "down": pairs(lambda r, x: (r, x - 1) if x > 0 else None),
        "cross": ends(lambda r: (r - 1, last), lambda r: (r + 1, 0)),
        "far": ends(lambda r: (r + 1, 0), lambda r: (r - 1, last)),
        "inward": ends(lambda r: (r, 1), lambda r: (r, last - 1)),
        "outward": pairs(
            lambda r, x: (r - 1, last) if x == 1 else (r + 1, 0) if x == last - 1 else None
        ),
    }


def device_work(query_rows, key_rows, value_rows, attn_output, out_grad, neighbours, counts):
    seq_rows, batch, width = out_grad.shape
    shard_tokens, _, head_dim = query_rows.shape
    nbr_count = neighbours.shape[1]
    tiles_all = counts.shape[0]
    tiles_dev = shard_tokens // TILE
    half = shard_tokens // 2
    peers = shard_tokens // seq_rows
    ring_len = 4
    route = routes(lax.axis_size("seq"), ring_len)
    shard = lax.axis_index("seq").astype(jnp.int32)
    at_start = lax.rem(shard, ring_len) == 0

    def move(rows, name):
        return lax.ppermute(rows, "seq", route[name])

    def edge(rows):
        return jnp.where(at_start, rows[:half], rows[half:])

    q = query_rows.reshape(shard_tokens, head_dim)
    k = key_rows.reshape(shard_tokens, head_dim)
    v = value_rows.reshape(shard_tokens, head_dim)
    o = attn_output.reshape(shard_tokens, head_dim)
    table = neighbours.reshape(-1)
    sent = out_grad.reshape(seq_rows, peers, head_dim).transpose(1, 0, 2)
    grads = lax.all_to_all(sent, "head", split_axis=0, concat_axis=0, tiled=True)
    grads = grads.reshape(shard_tokens, head_dim)
    kv_low = move(jnp.concatenate([k[half:], v[half:]]), "around")
    kv_high = move(jnp.concatenate([k[:half], v[:half]]), "around_back")
    k_far = move(edge(k), "cross")
    q_side = move(edge(q), "inward")
    v_far = move(jnp.where(at_start, kv_low[half:], kv_high[half:]), "far")
    q_far = move(q_side, "outward")
    g_far = move(edge(grads), "cross")
    qg_low = move(jnp.concatenate([q[half:], grads[half:]]), "up")
    qg_high = move(jnp.concatenate([q[:half], grads[:half]]), "down")

    smem = pl.BlockSpec(memory_space=pltpu.SMEM)
    vmem = pl.BlockSpec(memory_space=pltpu.VMEM)
    hbm = pl.BlockSpec(memory_space=pl.ANY)
    stat = jax.ShapeDtypeStruct((tiles_dev, head_dim), jnp.float32)
    held = pltpu.VMEM((shard_tokens, head_dim), jnp.bfloat16)
    wide = pltpu.VMEM((2 * shard_tokens, head_dim), jnp.bfloat16)
    acc = pltpu.VMEM((shard_tokens + TILE, head_dim), jnp.float32)
    place = shard.reshape(1)
    stat_all, stat_low, stat_high = pl.pallas_call(
        stats_kernel(tiles_dev, nbr_count, ring_len),
        out_shape=(
            jax.ShapeDtypeStruct((2 * tiles_dev, head_dim), jnp.float32), stat, stat,
        ),
        in_specs=[smem] * 3 + [hbm] * 7,
        out_specs=(vmem,) * 3,
        scratch_shapes=[held, held, held, wide, pltpu.SemaphoreType.DMA((6,))],
        name="rowstats",
    )(place, table, counts, q, k, o, grads, kv_low, kv_high, k_far)
    near_low = move(stat_high, "forward")
    near_high = move(stat_low, "backward")
    joint = pl.pallas_call(
        grads_kernel(tiles_dev, tiles_all, nbr_count, ring_len, peers),
        out_shape=jax.ShapeDtypeStruct((peers, 3, seq_rows, head_dim), jnp.bfloat16),
        in_specs=[smem] * 3 + [hbm] * 15,
        out_specs=vmem,
        scratch_shapes=[
            held, held, wide, wide, held, held, acc, acc,
            pltpu.VMEM((2 * tiles_dev, head_dim), jnp.float32),
            pltpu.VMEM((2, tiles_dev, head_dim), jnp.float32),
            pltpu.SMEM((2, tiles_dev * nbr_count), jnp.int32),
            pltpu.SemaphoreType.DMA((15,)),
        ],
        name="gradsum",
    )(
        place, table, counts, q, k, v, grads, kv_low, kv_high, k_far, v_far,
        qg_low, qg_high, q_far, g_far, stat_all, near_low, near_high,
    )
    back = lax.all_to_all(joint, "head", split_axis=0, concat_axis=0, tiled=True)

    def to_rows(block):
        return block.transpose(1, 0, 2).reshape(seq_rows, batch, width)

    return to_rows(back[:, 0]), to_rows(back[:, 1]), to_rows(back[:, 2])


def solution(mesh):
    placed = (
        P("seq", "head", None),
        P("seq", "head", None),
        P("seq", "head", None),
        P("seq", "head", None),
        P(("seq", "head"), None, None),
        P(),
        P(),
    )
    return jax.shard_map(
        device_work,
        mesh=mesh,
        in_specs=placed,
        out_specs=(
            P(("seq", "head"), None, None),
            P(("seq", "head"), None, None),
            P(("seq", "head"), None, None),
        ),
        check_vma=False,
    )
```

time: 197 us -> 170 us (0.86)
  waiting for transfers between devices: 81.9 us -> 14.3 us
  blocking collectives: 0 us -> 57.4 us
  starting transfers between devices: 80.7 us -> 62.5 us
  other arithmetic: 0.06 us -> 3.41 us
    all_to_all x0 -> x1, blocking collectives: none -> 57.4 us  [device_work(): lax.all_to_all(joint, 'head', split_axis=0, concat_axis=0, tiled=True)]
    ppermute x12 -> x11, waiting for transfers between devices: 54.4 us -> 14.3 us  [move(): return lax.ppermute(rows, 'seq', route[name])]
    all_to_all x2 -> x0, waiting for transfers between devices: 27.5 us -> none  [the longest x1 27.5 us: device_work(): lax.all_to_all(joint, 'head', split_axis=0, concat_axis=0, tiled=True)]
    all_to_all x2 -> x0, starting transfers between devices: 19 us -> none  [the longest x1 10 us: device_work(): lax.all_to_all(dq.reshape(peers, seq_rows, head_dim), 'head', split_axis=...]
    concatenate x0 -> x4, other arithmetic: none -> 2.55 us  [the longest x1 0.86 us: device_work(): qg_high = move(jnp.concatenate([q[:half], grads[:half]]), 'down')]
    ppermute x12 -> x11, starting transfers between devices: 47.8 us -> 48.7 us  [move(): return lax.ppermute(rows, 'seq', route[name])]
  transfers between devices with their start and end apart: 15 -> 12, of which waited for: 7 -> 3; matrix products, arithmetic and copies ran while one was open for 1% -> 3% of each run, Pallas kernels for 3% -> 4%
where the time goes in v3:
time: 170 us; the launch traced here: 169 us
  starting transfers between devices  62.5 us (37%)
  blocking collectives  57.4 us (34%)
  Pallas kernels  22.4 us (13%)
  waiting for transfers between devices  14.3 us (8%)
  local copies, waits for them, and re-layouts  8.09 us (5%)
  other arithmetic  3.41 us (2%)
    all_to_all x1, blocking collectives, device_work(): lax.all_to_all(joint, 'head', split_axis=0, concat_axis=0, tiled=True)  57.4 us
    ppermute x11, starting transfers between devices, move(): return lax.ppermute(rows, 'seq', route[name])  48.7 us
    pallas_call x1, Pallas kernels, device_work(): pl.pallas_call(grads_kernel(tiles_dev, tiles_all, nbr_count, ring_len, pe...  16.2 us
    ppermute x11, waiting for transfers between devices, move(): return lax.ppermute(rows, 'seq', route[name])  14.3 us
    all_to_all x1, starting transfers between devices, device_work(): lax.all_to_all(sent, 'head', split_axis=0, concat_axis=0, tiled=True)  13.8 us
    pallas_call x1, Pallas kernels, device_work(): pl.pallas_call(stats_kernel(tiles_dev, nbr_count, ring_len), out_shape=(j...  6.21 us
  transfers between devices with their start and end apart: 12, of which 3 were waited for; matrix products, arithmetic and copies ran while one was open for 3% of the time, Pallas kernels for 4%

profile of v3, /device:TPU:7, one launch (start us, length us, event | category | flops | bytes accessed | tf_op | source)
XLA Modules:
  0.0 169.1 jit_solution(1666227194261557753)
XLA Ops:
  0.6 1.4 reshape.52
  2.1 1.1 copy.17
  3.2 13.8 %all-to-all-start = ((bf16[64,32,128]{2,1,0:T(8,128)(2,1)}), bf16[64,32,128]{2,1,0:T(8,128)(2,1)S(1)}, u32[]{:S(2)}, u32[]{:S(2)}) async-start(bf16[64,32,128]{2,1,0:T(8,128)(2,1)} %bitcast.44), calls=%async_computation | async-start | bytes 1048576 | tf_op jit(solution)/shard_map/all_to_all | solution.py:309
  17.8 10.2 %collective-permute-start.2 = (bf16[1024,128]{1,0:T(8,128)(2,1)}, bf16[1024,128]{1,0:T(8,128)(2,1)S(1)}, u32[]{:S(2)}, u32[]{:S(2)}) collective-permute-start(bf16[1024,128]{1,0:T(8,128)(2,1)} %broadcast_select_fusion.2), channel_id=1, source_target_pairs={{192,256},{256,192},{448,512},{512,448},{193,257},{257,193},{449,5... | collective-permute-start | bytes 786440 | tf_op jit(solution)/shard_map/ppermute | solution.py:298
  28.1 2.0 %collective-permute-start.6 = (bf16[1024,128]{1,0:T(8,128)(2,1)S(1)}, bf16[1024,128]{1,0:T(8,128)(2,1)}, u32[]{:S(2)}, u32[]{:S(2)}) collective-permute-start(bf16[1024,128]{1,0:T(8,128)(2,1)S(1)} %broadcast_select_fusion.1), channel_id=1, source_target_pairs={{0,64},{192,128},{256,320},{448,384},{512,576},{704,640},{1,65},{1... | collective-permute-start | bytes 786440 | tf_op jit(solution)/shard_map/ppermute | solution.py:298
  30.2 0.8 pad_maximum_fusion
  31.0 1.9 %collective-permute-start = (bf16[2048,128]{1,0:T(8,128)(2,1)}, bf16[2048,128]{1,0:T(8,128)(2,1)S(1)}, u32[]{:S(2)}, u32[]{:S(2)}) collective-permute-start(bf16[2048,128]{1,0:T(8,128)(2,1)} %pad_maximum_fusion), channel_id=1, source_target_pairs={{0,64},{64,128},{128,192},{192,0},{256,320},{320,384},{384,448},{4... | collective-permute-start | bytes 1572872 | tf_op jit(solution)/shard_map/ppermute | solution.py:298
  33.7 3.3 %collective-permute-start.1 = (bf16[2048,128]{1,0:T(8,128)(2,1)}, bf16[2048,128]{1,0:T(8,128)(2,1)S(1)}, u32[]{:S(2)}, u32[]{:S(2)}) collective-permute-start(bf16[2048,128]{1,0:T(8,128)(2,1)} %pad_maximum_fusion.1), channel_id=1, source_target_pairs={{0,192},{64,0},{128,64},{192,128},{256,448},{320,256},{384,320},{4... | collective-permute-start | bytes 1572872 | tf_op jit(solution)/shard_map/ppermute | solution.py:298
  37.1 1.3 collective-permute-start.7
  38.6 1.4 collective-permute-start.4
  40.0 0.9 pad_maximum_fusion.3
  40.9 5.0 %collective-permute-done.kv_lo = bf16[2048,128]{1,0:T(8,128)(2,1)S(1)} collective-permute-done((bf16[2048,128]{1,0:T(8,128)(2,1)}, bf16[2048,128]{1,0:T(8,128)(2,1)S(1)}, u32[]{:S(2)}, u32[]{:S(2)}) %collective-permute-start) | collective-permute-done | bytes 524320 | tf_op jit(solution)/shard_map/ppermute | solution.py:298
  45.8 4.3 %collective-permute-start.5 = (bf16[2048,128]{1,0:T(8,128)(2,1)}, bf16[2048,128]{1,0:T(8,128)(2,1)S(1)}, u32[]{:S(2)}, u32[]{:S(2)}) collective-permute-start(bf16[2048,128]{1,0:T(8,128)(2,1)} %pad_maximum_fusion.3), channel_id=1, source_target_pairs={{64,0},{128,64},{192,128},{320,256},{384,320},{448,384},{576,512},... | collective-permute-start | bytes 1572872 | tf_op jit(solution)/shard_map/ppermute | solution.py:298
  51.0 1.3 collective-permute-start.3
  52.4 17.6 %collective-permute-start.8 = (bf16[1024,128]{1,0:T(8,128)(2,1)S(1)}, bf16[1024,128]{1,0:T(8,128)(2,1)S(1)}, u32[]{:S(2)}, u32[]{:S(2)}) collective-permute-start(bf16[1024,128]{1,0:T(8,128)(2,1)S(1)} %broadcast_select_fusion), channel_id=1, source_target_pairs={{192,256},{256,192},{448,512},{512,448},{193,257},{257,193},{449,5... | collective-permute-start | bytes 786440 | tf_op jit(solution)/shard_map/ppermute | solution.py:298
  70.8 6.2 %rowstats.1 = (f32[32,128]{1,0:T(8,128)}, f32[16,128]{1,0:T(8,128)}, f32[16,128]{1,0:T(8,128)}) custom-call(s32[1]{0:T(128)} %bitcast.shard, s32[768]{0:T(1024)} %reshape.48.nbr, s32[192]{0:T(256)} %cnt.3, bf16[2048,128]{1,0:T(8,128)(2,1)} %bitcast.45, bf16[2048,128]{1,0:T(8,128)(2,1)} %bitcast.47, bf16[2048,128]{1,0:T(8,128)(2,1)} %bitcast.54, ...), custom_call_target="tpu_custom_call" | custom-call | tf_op jit(solution)/shard_map/rowstats/pallas_call | solution.py:329
  77.0 1.9 %collective-permute-start.9 = (f32[16,128]{1,0:T(8,128)}, f32[16,128]{1,0:T(8,128)S(1)}, u32[]{:S(2)}, u32[]{:S(2)}) collective-permute-start(f32[16,128]{1,0:T(8,128)} %get-tuple-element.7), channel_id=1, source_target_pairs={{0,64},{64,128},{128,192},{192,256},{256,320},{320,384},{384,448},... | collective-permute-start | bytes 24584 | tf_op jit(solution)/shard_map/ppermute | solution.py:298
  79.0 3.4 %collective-permute-start.10 = (f32[16,128]{1,0:T(8,128)}, f32[16,128]{1,0:T(8,128)S(1)}, u32[]{:S(2)}, u32[]{:S(2)}) collective-permute-start(f32[16,128]{1,0:T(8,128)} %get-tuple-element.8), channel_id=1, source_target_pairs={{64,0},{128,64},{192,128},{256,192},{320,256},{384,320},{448,384},... | collective-permute-start | bytes 24584 | tf_op jit(solution)/shard_map/ppermute | solution.py:298
  82.4 8.5 %collective-permute-done.10.shi = f32[16,128]{1,0:T(8,128)S(1)} collective-permute-done((f32[16,128]{1,0:T(8,128)}, f32[16,128]{1,0:T(8,128)S(1)}, u32[]{:S(2)}, u32[]{:S(2)}) %collective-permute-start.10) | collective-permute-done | bytes 8224 | tf_op jit(solution)/shard_map/ppermute | solution.py:298
  91.8 16.2 %gradsum.1 = bf16[64,3,32,128]{3,2,1,0:T(8,128)(2,1)} custom-call(s32[1]{0:T(128)} %bitcast.shard, s32[768]{0:T(1024)} %reshape.48.nbr, s32[192]{0:T(256)} %cnt.3, bf16[2048,128]{1,0:T(8,128)(2,1)} %bitcast.46, bf16[2048,128]{1,0:T(8,128)(2,1)} %bitcast.48, bf16[2048,128]{1,0:T(8,128)(2,1)} %bitcast.53, bf16[2048,128]{1,0:T(8,128)(2,1)} %bitcast.50, ...), custom_call_target="tpu_custom_call" | custom-call | tf_op jit(solution)/shard_map/gradsum/pallas_call | solution.py:341
  108.0 57.4 %all_to_all.10 = bf16[64,3,32,128]{3,2,1,0:T(8,128)(2,1)S(1)} all-to-all(bf16[64,3,32,128]{3,2,1,0:T(8,128)(2,1)} %gradsum.1), channel_id=1, replica_groups=mesh['seq'=12,'head'=64] {'head'}, dimensions={0} | all-to-all | bytes 3145728 | tf_op jit(solution)/shard_map/all_to_all | solution.py:358
  165.9 0.9 reshape.57
  167.1 0.9 reshape.56
  168.2 0.9 reshape.55
  (50 shorter events, 5.3 us)
Async XLA Ops:
  0.6 16.4 %copy-start.1 = (bf16[2048,1,128]{2,0,1:T(8,128)(2,1)S(1)}, bf16[2048,1,128]{2,0,1:T(8,128)(2,1)}, u32[]{:S(2)}) copy-start(bf16[2048,1,128]{2,0,1:T(8,128)(2,1)} %param.8) | copy-start | bytes 1572868
  2.1 25.9 %copy-start = (bf16[2048,1,128]{2,0,1:T(8,128)(2,1)S(1)}, bf16[2048,1,128]{2,0,1:T(8,128)(2,1)}, u32[]{:S(2)}) copy-start(bf16[2048,1,128]{2,0,1:T(8,128)(2,1)} %param.7) | copy-start | bytes 1572868
  3.2 35.2 %all-to-all-start = ((bf16[64,32,128]{2,1,0:T(8,128)(2,1)}), bf16[64,32,128]{2,1,0:T(8,128)(2,1)S(1)}, u32[]{:S(2)}, u32[]{:S(2)}) async-start(bf16[64,32,128]{2,1,0:T(8,128)(2,1)} %bitcast.44), calls=%async_computation | async-start | bytes 1048576 | tf_op jit(solution)/shard_map/all_to_all | solution.py:309
  17.0 13.1 %copy-start.5 = (bf16[2048,1,128]{2,0,1:T(8,128)(2,1)S(1)}, bf16[2048,1,128]{2,0,1:T(8,128)(2,1)}, u32[]{:S(2)}) copy-start(bf16[2048,1,128]{2,0,1:T(8,128)(2,1)} %param.9) | copy-start | bytes 1572868
  17.8 34.6 %collective-permute-start.2 = (bf16[1024,128]{1,0:T(8,128)(2,1)}, bf16[1024,128]{1,0:T(8,128)(2,1)S(1)}, u32[]{:S(2)}, u32[]{:S(2)}) collective-permute-start(bf16[1024,128]{1,0:T(8,128)(2,1)} %broadcast_select_fusion.2), channel_id=1, source_target_pairs={{192,256},{256,192},{448,512},{512,448},{193,257},{257,193},{449,5... | collective-permute-start | bytes 786440 | tf_op jit(solution)/shard_map/ppermute | solution.py:298
  28.1 9.1 %collective-permute-start.6 = (bf16[1024,128]{1,0:T(8,128)(2,1)S(1)}, bf16[1024,128]{1,0:T(8,128)(2,1)}, u32[]{:S(2)}, u32[]{:S(2)}) collective-permute-start(bf16[1024,128]{1,0:T(8,128)(2,1)S(1)} %broadcast_select_fusion.1), channel_id=1, source_target_pairs={{0,64},{192,128},{256,320},{448,384},{512,576},{704,640},{1,65},{1... | collective-permute-start | bytes 786440 | tf_op jit(solution)/shard_map/ppermute | solution.py:298
  31.0 14.8 %collective-permute-start = (bf16[2048,128]{1,0:T(8,128)(2,1)}, bf16[2048,128]{1,0:T(8,128)(2,1)S(1)}, u32[]{:S(2)}, u32[]{:S(2)}) collective-permute-start(bf16[2048,128]{1,0:T(8,128)(2,1)} %pad_maximum_fusion), channel_id=1, source_target_pairs={{0,64},{64,128},{128,192},{192,0},{256,320},{320,384},{384,448},{4... | collective-permute-start | bytes 1572872 | tf_op jit(solution)/shard_map/ppermute | solution.py:298
  33.7 17.2 %collective-permute-start.1 = (bf16[2048,128]{1,0:T(8,128)(2,1)}, bf16[2048,128]{1,0:T(8,128)(2,1)S(1)}, u32[]{:S(2)}, u32[]{:S(2)}) collective-permute-start(bf16[2048,128]{1,0:T(8,128)(2,1)} %pad_maximum_fusion.1), channel_id=1, source_target_pairs={{0,192},{64,0},{128,64},{192,128},{256,448},{320,256},{384,320},{4... | collective-permute-start | bytes 1572872 | tf_op jit(solution)/shard_map/ppermute | solution.py:298
  37.1 39.9 %collective-permute-start.7 = (bf16[1024,128]{1,0:T(8,128)(2,1)}, bf16[1024,128]{1,0:T(8,128)(2,1)}, u32[]{:S(2)}, u32[]{:S(2)}) collective-permute-start(bf16[1024,128]{1,0:T(8,128)(2,1)} %collective-permute-done.6), channel_id=1, source_target_pairs={{128,256},{320,192},{384,512},{576,448},{129,257},{321,193},{385,5... | collective-permute-start | bytes 786440 | tf_op jit(solution)/shard_map/ppermute | solution.py:298
  38.5 2.4 %copy-start.2 = (bf16[64,32,128]{2,1,0:T(8,128)(2,1)}, bf16[64,32,128]{2,1,0:T(8,128)(2,1)S(1)}, u32[]{:S(2)}) copy-start(bf16[64,32,128]{2,1,0:T(8,128)(2,1)S(1)} %all-to-all-done) | copy-start | bytes 1572868
  38.6 31.4 %copy-start.11 = (s32[192,4]{0,1:T(4,128)S(1)}, s32[192,4]{0,1:T(4,128)}, u32[]{:S(2)}) copy-start(s32[192,4]{0,1:T(4,128)} %param.12) | copy-start | bytes 9220
  38.6 52.3 %collective-permute-start.4 = (bf16[2048,128]{1,0:T(8,128)(2,1)S(1)}, bf16[2048,128]{1,0:T(8,128)(2,1)}, u32[]{:S(2)}, u32[]{:S(2)}) collective-permute-start(bf16[2048,128]{1,0:T(8,128)(2,1)S(1)} %pad_maximum_fusion.2), channel_id=1, source_target_pairs={{0,64},{64,128},{128,192},{256,320},{320,384},{384,448},{512,576},... | collective-permute-start | bytes 1572872 | tf_op jit(solution)/shard_map/ppermute | solution.py:298
  45.8 25.0 %copy-start.3 = (bf16[2048,128]{1,0:T(8,128)(2,1)}, bf16[2048,128]{1,0:T(8,128)(2,1)S(1)}, u32[]{:S(2)}) copy-start(bf16[2048,128]{1,0:T(8,128)(2,1)S(1)} %collective-permute-done.kv_lo) | copy-start | bytes 1572868
  45.8 45.1 %collective-permute-start.5 = (bf16[2048,128]{1,0:T(8,128)(2,1)}, bf16[2048,128]{1,0:T(8,128)(2,1)S(1)}, u32[]{:S(2)}, u32[]{:S(2)}) collective-permute-start(bf16[2048,128]{1,0:T(8,128)(2,1)} %pad_maximum_fusion.3), channel_id=1, source_target_pairs={{64,0},{128,64},{192,128},{320,256},{384,320},{448,384},{576,512},... | collective-permute-start | bytes 1572872 | tf_op jit(solution)/shard_map/ppermute | solution.py:298
  51.0 19.9 %copy-start.4 = (bf16[2048,128]{1,0:T(8,128)(2,1)}, bf16[2048,128]{1,0:T(8,128)(2,1)S(1)}, u32[]{:S(2)}) copy-start(bf16[2048,128]{1,0:T(8,128)(2,1)S(1)} %collective-permute-done.1.kv_hi) | copy-start | bytes 1572868
  51.0 28.0 %collective-permute-start.3 = (bf16[1024,128]{1,0:T(8,128)(2,1)S(1)}, bf16[1024,128]{1,0:T(8,128)(2,1)}, u32[]{:S(2)}, u32[]{:S(2)}) collective-permute-start(bf16[1024,128]{1,0:T(8,128)(2,1)S(1)} %slice_select_fusion), channel_id=1, source_target_pairs={{0,256},{256,512},{448,192},{704,448},{1,257},{257,513},{449,193},... | collective-permute-start | bytes 786440 | tf_op jit(solution)/shard_map/ppermute | solution.py:298
  52.4 18.4 %copy-start.6 = (bf16[1024,128]{1,0:T(8,128)(2,1)}, bf16[1024,128]{1,0:T(8,128)(2,1)S(1)}, u32[]{:S(2)}) copy-start(bf16[1024,128]{1,0:T(8,128)(2,1)S(1)} %collective-permute-done.2.kz) | copy-start | bytes 786436
  52.4 38.5 %collective-permute-start.8 = (bf16[1024,128]{1,0:T(8,128)(2,1)S(1)}, bf16[1024,128]{1,0:T(8,128)(2,1)S(1)}, u32[]{:S(2)}, u32[]{:S(2)}) collective-permute-start(bf16[1024,128]{1,0:T(8,128)(2,1)S(1)} %broadcast_select_fusion), channel_id=1, source_target_pairs={{192,256},{256,192},{448,512},{512,448},{193,257},{257,193},{449,5... | collective-permute-start | bytes 786440 | tf_op jit(solution)/shard_map/ppermute | solution.py:298
  77.0 5.3 %collective-permute-start.9 = (f32[16,128]{1,0:T(8,128)}, f32[16,128]{1,0:T(8,128)S(1)}, u32[]{:S(2)}, u32[]{:S(2)}) collective-permute-start(f32[16,128]{1,0:T(8,128)} %get-tuple-element.7), channel_id=1, source_target_pairs={{0,64},{64,128},{128,192},{192,256},{256,320},{320,384},{384,448},... | collective-permute-start | bytes 24584 | tf_op jit(solution)/shard_map/ppermute | solution.py:298
  79.0 11.9 %collective-permute-start.10 = (f32[16,128]{1,0:T(8,128)}, f32[16,128]{1,0:T(8,128)S(1)}, u32[]{:S(2)}, u32[]{:S(2)}) collective-permute-start(f32[16,128]{1,0:T(8,128)} %get-tuple-element.8), channel_id=1, source_target_pairs={{64,0},{128,64},{192,128},{256,192},{320,256},{384,320},{448,384},... | collective-permute-start | bytes 24584 | tf_op jit(solution)/shard_map/ppermute | solution.py:298
  82.4 8.6 %copy-start.9 = (f32[16,128]{1,0:T(8,128)}, f32[16,128]{1,0:T(8,128)S(1)}, u32[]{:S(2)}) copy-start(f32[16,128]{1,0:T(8,128)S(1)} %collective-permute-done.9.slo) | copy-start | bytes 24580
  90.9 0.6 copy-start.10
  90.9 0.7 copy-start.8
  90.9 0.9 copy-start.7

commit v4 on v3

--- a/solution.py
+++ b/solution.py
@@ -49,7 +49,7 @@
     scale_two = TILE ** (-0.5) * math.log2(math.e)
 
     def kernel(
-        shard, nbr, cnt, q_any, k_any, o_any, g_any, kv_lo, kv_hi, kz,
+        shard, nbr, cnt, q_any, k_any, o_any, g_any, k_lo, k_hi, kz,
         stat_all, stat_lo, stat_hi,
         q, o, g, k_ext, sems,
     ):
@@ -62,11 +62,8 @@
             (q, (q_any,)),
             (o, (o_any,)),
             (g, (g_any,)),
-            (k_ext.at[pl.ds(0, half)], (kz, col == 0, kv_lo.at[pl.ds(0, half)])),
-            (
-                k_ext.at[pl.ds(half + own, half)],
-                (kz, col == ring_len - 1, kv_hi.at[pl.ds(0, half)]),
-            ),
+            (k_ext.at[pl.ds(0, half)], (kz, col == 0, k_lo)),
+            (k_ext.at[pl.ds(half + own, half)], (kz, col == ring_len - 1, k_hi)),
         )
         start_copies(moves, sems)
         wait_copies(moves, sems)
@@ -122,8 +119,8 @@
     scale_two = scale * math.log2(math.e)
 
     def kernel(
-        shard, nbr, cnt, q_any, k_any, v_any, g_any, kv_lo, kv_hi, kz, vz,
-        qg_lo, qg_hi, qz, gz, stat_any, slo, shi,
+        shard, nbr, cnt, q_any, k_any, v_any, g_any, k_lo, k_hi, kz,
+        lo, hi, vz, qz, gz, stat_any, slo, shi,
         joint, q, g, k_ext, v_ext, q_near, g_near, dk_acc, dv_acc, stats, stats_near, pairs, sems,
     ):
         s = shard[0]
@@ -134,6 +131,7 @@
         at_high = col == ring_len - 1
         first_half = pl.ds(0, half)
         second_half = pl.ds(half, half)
+        third_half = pl.ds(2 * half, half)
         above = pl.ds(half + own, half)
         moves = (
             (k_ext.at[pl.ds(half, own)], (k_any,)),
@@ -143,14 +141,14 @@
             (stats, (stat_any,)),
             (stats_near.at[0], (slo,)),
             (stats_near.at[1], (shi,)),
-            (k_ext.at[first_half], (kz, at_low, kv_lo.at[first_half])),
-            (k_ext.at[above], (kz, at_high, kv_hi.at[first_half])),
-            (v_ext.at[first_half], (vz, at_low, kv_lo.at[second_half])),
-            (v_ext.at[above], (vz, at_high, kv_hi.at[second_half])),
-            (q_near.at[first_half], (qz, at_low, qg_lo.at[first_half])),
-            (q_near.at[second_half], (qz, at_high, qg_hi.at[first_half])),
-            (g_near.at[first_half], (gz, at_low, qg_lo.at[second_half])),
-            (g_near.at[second_half], (gz, at_high, qg_hi.at[second_half])),
+            (k_ext.at[first_half], (kz, at_low, k_lo)),
+            (k_ext.at[above], (kz, at_high, k_hi)),
+            (v_ext.at[first_half], (vz, at_low, lo.at[first_half])),
+            (v_ext.at[above], (vz, at_high, hi.at[first_half])),
+            (q_near.at[first_half], (qz, at_low, lo.at[second_half])),
+            (q_near.at[second_half], (qz, at_high, hi.at[second_half])),
+            (g_near.at[first_half], (gz, at_low, lo.at[third_half])),
+            (g_near.at[second_half], (gz, at_high, hi.at[third_half])),
         )
         start_copies(moves, sems)
         zero = jnp.zeros((own, TILE), jnp.float32)
@@ -189,7 +187,7 @@
             dscore = (prob * (dprob - delta) * scale).astype(jnp.bfloat16)
             return key, prob.astype(jnp.bfloat16), dscore
 
-        def own_step(t, carry):
+        def own_terms(t):
             tile = first_tile + t
             q_t = q[span(t), :]
             g_t = queries(g, t, tile)
@@ -205,17 +203,25 @@
                 keys.append(key)
                 probs.append(prob)
                 dscores.append(dscore)
+            return t, q_t, g_t, places, keys, probs, dscores
+
+        def own_sums(t, q_t, g_t, places, keys, probs, dscores):
+            for mine, dscore, prob in zip(places, dscores, probs):
+                dk_acc[span(mine), :] += dot(dscore, q_t, NN)
+                dv_acc[span(mine), :] += dot(prob, g_t, NN)
             dq = dot(jnp.concatenate(dscores), jnp.concatenate(keys), TN)
-            sums = [(dot(ds, q_t, NN), dot(pb, g_t, NN)) for ds, pb in zip(dscores, probs)]
-            for mine, (dk, dv) in zip(places, sums):
-                dk_acc[span(mine), :] += dk
-                dv_acc[span(mine), :] += dv
             joint[pl.ds(t * tile_peers, tile_peers), 0] = (
                 dq.astype(jnp.bfloat16).reshape(tile_peers, share, TILE)
             )
+
+        def own_step(i, carry):
+            first = own_terms(2 * i)
+            second = own_terms(2 * i + 1)
+            own_sums(*first)
+            own_sums(*second)
             return carry
 
-        lax.fori_loop(0, tiles_dev, own_step, 0)
+        lax.fori_loop(0, tiles_dev // 2, own_step, 0)
 
         def near_terms(index):
             i = pairs[0, index]
@@ -275,6 +281,10 @@
         "cross": ends(lambda r: (r - 1, last), lambda r: (r + 1, 0)),
         "far": ends(lambda r: (r + 1, 0), lambda r: (r - 1, last)),
         "inward": ends(lambda r: (r, 1), lambda r: (r, last - 1)),
+        "inward_two": ends(lambda r: (r, last - 1), lambda r: (r, 1)),
+        "outward_two": pairs(
+            lambda r, x: (r + 1, 0) if x == 1 else (r - 1, last) if x == last - 1 else None
+        ),
         "outward": pairs(
             lambda r, x: (r - 1, last) if x == 1 else (r + 1, 0) if x == last - 1 else None
         ),
@@ -308,15 +318,16 @@
     sent = out_grad.reshape(seq_rows, peers, head_dim).transpose(1, 0, 2)
     grads = lax.all_to_all(sent, "head", split_axis=0, concat_axis=0, tiled=True)
     grads = grads.reshape(shard_tokens, head_dim)
-    kv_low = move(jnp.concatenate([k[half:], v[half:]]), "around")
-    kv_high = move(jnp.concatenate([k[:half], v[:half]]), "around_back")
-    k_far = move(edge(k), "cross")
+    k_low = move(k[half:], "around")
+    k_high = move(k[:half], "around_back")
     q_side = move(edge(q), "inward")
-    v_far = move(jnp.where(at_start, kv_low[half:], kv_high[half:]), "far")
+    v_side = move(edge(v), "inward_two")
+    k_far = move(jnp.where(at_start, k_low, k_high), "far")
     q_far = move(q_side, "outward")
+    v_far = move(v_side, "outward_two")
     g_far = move(edge(grads), "cross")
-    qg_low = move(jnp.concatenate([q[half:], grads[half:]]), "up")
-    qg_high = move(jnp.concatenate([q[:half], grads[:half]]), "down")
+    low = move(jnp.concatenate([v[half:], q[half:], grads[half:]]), "up")
+    high = move(jnp.concatenate([v[:half], q[:half], grads[:half]]), "down")
 
     smem = pl.BlockSpec(memory_space=pltpu.SMEM)
     vmem = pl.BlockSpec(memory_space=pltpu.VMEM)
@@ -335,7 +346,7 @@
         out_specs=(vmem,) * 3,
         scratch_shapes=[held, held, held, wide, pltpu.SemaphoreType.DMA((6,))],
         name="rowstats",
-    )(place, table, counts, q, k, o, grads, kv_low, kv_high, k_far)
+    )(place, table, counts, q, k, o, grads, k_low, k_high, k_far)
     near_low = move(stat_high, "forward")
     near_high = move(stat_low, "backward")
     joint = pl.pallas_call(
@@ -352,8 +363,8 @@
         ],
         name="gradsum",
     )(
-        place, table, counts, q, k, v, grads, kv_low, kv_high, k_far, v_far,
-        qg_low, qg_high, q_far, g_far, stat_all, near_low, near_high,
+        place, table, counts, q, k, v, grads, k_low, k_high, k_far,
+        low, high, v_far, q_far, g_far, stat_all, near_low, near_high,
     )
     back = lax.all_to_all(joint, "head", split_axis=0, concat_axis=0, tiled=True)
 

time: 170 us -> 175 us (1.029)
  waiting for transfers between devices: 14.3 us -> 46.1 us
  starting transfers between devices: 62.5 us -> 48.9 us
  blocking collectives: 57.4 us -> 49.1 us
  Pallas kernels: 22.4 us -> 18.7 us
    ppermute x11 -> x12, waiting for transfers between devices: 14.3 us -> 41 us  [move(): return lax.ppermute(rows, 'seq', route[name])]
    ppermute x11 -> x12, starting transfers between devices: 48.7 us -> 35.1 us  [move(): return lax.ppermute(rows, 'seq', route[name])]
    all_to_all x1, blocking collectives: 57.4 us -> 49.1 us  [device_work(): lax.all_to_all(joint, 'head', split_axis=0, concat_axis=0, tiled=True)]
    all_to_all x1, waiting for transfers between devices: 0.01 us -> 5.12 us  [device_work(): lax.all_to_all(sent, 'head', split_axis=0, concat_axis=0, tiled=True)]
    pallas_call x1, Pallas kernels: 16.2 us -> 12.5 us  [device_work(): pl.pallas_call(grads_kernel(tiles_dev, tiles_all, nbr_count, ring_len, pe...]
  transfers between devices with their start and end apart: 12 -> 13, of which waited for: 3 -> 5; matrix products, arithmetic and copies ran while one was open for 3% -> 2% of each run, Pallas kernels for 4% -> 4%
where the time goes in v4:
time: 175 us; the launch traced here: 174 us
  blocking collectives  49.1 us (28%)
  starting transfers between devices  48.9 us (28%)
  waiting for transfers between devices  46.1 us (26%)
  Pallas kernels  18.7 us (11%)
  local copies, waits for them, and re-layouts  8.66 us (5%)
  other arithmetic  1.86 us (1%)
    all_to_all x1, blocking collectives, device_work(): lax.all_to_all(joint, 'head', split_axis=0, concat_axis=0, tiled=True)  49.1 us
    ppermute x12, waiting for transfers between devices, move(): return lax.ppermute(rows, 'seq', route[name])  41 us
    ppermute x12, starting transfers between devices, move(): return lax.ppermute(rows, 'seq', route[name])  35.1 us
    all_to_all x1, starting transfers between devices, device_work(): lax.all_to_all(sent, 'head', split_axis=0, concat_axis=0, tiled=True)  13.8 us
    pallas_call x1, Pallas kernels, device_work(): pl.pallas_call(grads_kernel(tiles_dev, tiles_all, nbr_count, ring_len, pe...  12.5 us
    pallas_call x1, Pallas kernels, device_work(): pl.pallas_call(stats_kernel(tiles_dev, nbr_count, ring_len), out_shape=(j...  6.2 us
    all_to_all x1, waiting for transfers between devices, device_work(): lax.all_to_all(sent, 'head', split_axis=0, concat_axis=0, tiled=True)  5.12 us
  transfers between devices with their start and end apart: 13, of which 5 were waited for; matrix products, arithmetic and copies ran while one was open for 2% of the time, Pallas kernels for 4%

profile of v4, /device:TPU:7, one launch (start us, length us, event | category | flops | bytes accessed | tf_op | source)
XLA Modules:
  0.0 174.3 jit_solution(13120452848974289991)
XLA Ops:
  0.6 1.4 reshape.52
  2.1 1.1 copy.17
  3.2 13.8 %all-to-all-start = ((bf16[64,32,128]{2,1,0:T(8,128)(2,1)}), bf16[64,32,128]{2,1,0:T(8,128)(2,1)S(1)}, u32[]{:S(2)}, u32[]{:S(2)}) async-start(bf16[64,32,128]{2,1,0:T(8,128)(2,1)} %bitcast.44), calls=%async_computation | async-start | bytes 1048576 | tf_op jit(solution)/shard_map/all_to_all | solution.py:319
  17.8 3.8 %collective-permute-start.5 = (bf16[1024,128]{1,0:T(8,128)(2,1)}, bf16[1024,128]{1,0:T(8,128)(2,1)}, u32[]{:S(2)}, u32[]{:S(2)}) collective-permute-start(bf16[1024,128]{1,0:T(8,128)(2,1)} %broadcast_select_fusion.2), channel_id=1, source_target_pairs={{0,128},{192,64},{256,384},{448,320},{512,640},{704,576},{1,129},{... | collective-permute-start | bytes 786440 | tf_op jit(solution)/shard_map/ppermute | solution.py:308
  22.3 1.9 %collective-permute-start.1 = (bf16[1024,128]{1,0:T(8,128)(2,1)}, bf16[1024,128]{1,0:T(8,128)(2,1)S(1)}, u32[]{:S(2)}, u32[]{:S(2)}) collective-permute-start(bf16[1024,128]{1,0:T(8,128)(2,1)} %get-tuple-element.18), channel_id=1, source_target_pairs={{0,192},{64,0},{128,64},{192,128},{256,448},{320,256},{384,320},{4... | collective-permute-start | bytes 786440 | tf_op jit(solution)/shard_map/ppermute | solution.py:308
  24.3 4.6 %collective-permute-start = (bf16[1024,128]{1,0:T(8,128)(2,1)}, bf16[1024,128]{1,0:T(8,128)(2,1)S(1)}, u32[]{:S(2)}, u32[]{:S(2)}) collective-permute-start(bf16[1024,128]{1,0:T(8,128)(2,1)} %get-tuple-element.19), channel_id=1, source_target_pairs={{0,64},{64,128},{128,192},{192,0},{256,320},{320,384},{384,448},{4... | collective-permute-start | bytes 786440 | tf_op jit(solution)/shard_map/ppermute | solution.py:308
  28.9 5.1 %all-to-all-done = bf16[64,32,128]{2,1,0:T(8,128)(2,1)S(1)} async-done(((bf16[64,32,128]{2,1,0:T(8,128)(2,1)}), bf16[64,32,128]{2,1,0:T(8,128)(2,1)S(1)}, u32[]{:S(2)}, u32[]{:S(2)}) %all-to-all-start) | async-done | bytes 524320 | tf_op jit(solution)/shard_map/all_to_all | solution.py:319
  34.2 1.3 collective-permute-start.3
  35.5 0.9 pad_maximum_fusion.1
  36.4 5.0 %collective-permute-start.4 = (bf16[3072,128]{1,0:T(8,128)(2,1)}, bf16[3072,128]{1,0:T(8,128)(2,1)}, u32[]{:S(2)}, u32[]{:S(2)}) collective-permute-start(bf16[3072,128]{1,0:T(8,128)(2,1)} %pad_maximum_fusion.1), channel_id=1, source_target_pairs={{64,0},{128,64},{192,128},{320,256},{384,320},{448,384},{576,512},... | collective-permute-start | bytes 2359304 | tf_op jit(solution)/shard_map/ppermute | solution.py:308
  41.5 1.6 collective-permute-start.7
  43.1 1.3 collective-permute-start.2
  44.4 1.3 collective-permute-start.6
  45.7 16.8 %collective-permute-done.7 = bf16[1024,128]{1,0:T(8,128)(2,1)S(1)} collective-permute-done((bf16[1024,128]{1,0:T(8,128)(2,1)S(1)}, bf16[1024,128]{1,0:T(8,128)(2,1)S(1)}, u32[]{:S(2)}, u32[]{:S(2)}) %collective-permute-start.7) | collective-permute-done | bytes 262176 | tf_op jit(solution)/shard_map/ppermute | solution.py:308
  62.5 1.3 collective-permute-start.8
  63.9 12.0 %collective-permute-done.2.kz = bf16[1024,128]{1,0:T(8,128)(2,1)S(1)} collective-permute-done((bf16[1024,128]{1,0:T(8,128)(2,1)S(1)}, bf16[1024,128]{1,0:T(8,128)(2,1)S(1)}, u32[]{:S(2)}, u32[]{:S(2)}) %collective-permute-start.2) | collective-permute-done | bytes 262176 | tf_op jit(solution)/shard_map/ppermute | solution.py:308
  75.9 1.9 %collective-permute-start.9 = (bf16[1024,128]{1,0:T(8,128)(2,1)S(1)}, bf16[1024,128]{1,0:T(8,128)(2,1)S(1)}, u32[]{:S(2)}, u32[]{:S(2)}) collective-permute-start(bf16[1024,128]{1,0:T(8,128)(2,1)S(1)} %broadcast_select_fusion), channel_id=1, source_target_pairs={{192,256},{256,192},{448,512},{512,448},{193,257},{257,193},{449,5... | collective-permute-start | bytes 786440 | tf_op jit(solution)/shard_map/ppermute | solution.py:308
  78.7 6.2 %rowstats.1 = (f32[32,128]{1,0:T(8,128)}, f32[16,128]{1,0:T(8,128)}, f32[16,128]{1,0:T(8,128)}) custom-call(s32[1]{0:T(128)} %bitcast.shard, s32[768]{0:T(1024)} %reshape.48.nbr, s32[192]{0:T(256)} %cnt.3, bf16[2048,128]{1,0:T(8,128)(2,1)} %bitcast.45, bf16[2048,128]{1,0:T(8,128)(2,1)} %bitcast.50, bf16[2048,128]{1,0:T(8,128)(2,1)} %bitcast.54, ...), custom_call_target="tpu_custom_call" | custom-call | tf_op jit(solution)/shard_map/rowstats/pallas_call | solution.py:340
  84.9 9.3 %collective-permute-start.10 = (f32[16,128]{1,0:T(8,128)}, f32[16,128]{1,0:T(8,128)S(1)}, u32[]{:S(2)}, u32[]{:S(2)}) collective-permute-start(f32[16,128]{1,0:T(8,128)} %get-tuple-element.7), channel_id=1, source_target_pairs={{0,64},{64,128},{128,192},{192,256},{256,320},{320,384},{384,448},... | collective-permute-start | bytes 24584 | tf_op jit(solution)/shard_map/ppermute | solution.py:308
  94.3 2.2 %collective-permute-done.8.qz = bf16[1024,128]{1,0:T(8,128)(2,1)S(1)} collective-permute-done((bf16[1024,128]{1,0:T(8,128)(2,1)S(1)}, bf16[1024,128]{1,0:T(8,128)(2,1)S(1)}, u32[]{:S(2)}, u32[]{:S(2)}) %collective-permute-start.8) | collective-permute-done | bytes 262176 | tf_op jit(solution)/shard_map/ppermute | solution.py:308
  96.5 1.9 %collective-permute-start.11 = (f32[16,128]{1,0:T(8,128)}, f32[16,128]{1,0:T(8,128)S(1)}, u32[]{:S(2)}, u32[]{:S(2)}) collective-permute-start(f32[16,128]{1,0:T(8,128)} %get-tuple-element.8), channel_id=1, source_target_pairs={{64,0},{128,64},{192,128},{256,192},{320,256},{384,320},{448,384},... | collective-permute-start | bytes 24584 | tf_op jit(solution)/shard_map/ppermute | solution.py:308
  98.4 9.9 %collective-permute-done.11.shi = f32[16,128]{1,0:T(8,128)S(1)} collective-permute-done((f32[16,128]{1,0:T(8,128)}, f32[16,128]{1,0:T(8,128)S(1)}, u32[]{:S(2)}, u32[]{:S(2)}) %collective-permute-start.11) | collective-permute-done | bytes 8224 | tf_op jit(solution)/shard_map/ppermute | solution.py:308
  109.0 12.5 %gradsum.1 = bf16[64,3,32,128]{3,2,1,0:T(8,128)(2,1)} custom-call(s32[1]{0:T(128)} %bitcast.shard, s32[768]{0:T(1024)} %reshape.48.nbr, s32[192]{0:T(256)} %cnt.3, bf16[2048,128]{1,0:T(8,128)(2,1)} %bitcast.46, bf16[2048,128]{1,0:T(8,128)(2,1)} %bitcast.51, bf16[2048,128]{1,0:T(8,128)(2,1)} %bitcast.49, bf16[2048,128]{1,0:T(8,128)(2,1)} %bitcast.48, ...), custom_call_target="tpu_custom_call" | custom-call | tf_op jit(solution)/shard_map/gradsum/pallas_call | solution.py:352
  121.5 49.1 %all_to_all.10 = bf16[64,3,32,128]{3,2,1,0:T(8,128)(2,1)S(1)} all-to-all(bf16[64,3,32,128]{3,2,1,0:T(8,128)(2,1)} %gradsum.1), channel_id=1, replica_groups=mesh['seq'=12,'head'=64] {'head'}, dimensions={0} | all-to-all | bytes 3145728 | tf_op jit(solution)/shard_map/all_to_all | solution.py:369
  (52 shorter events, 7.0 us)
Async XLA Ops:
  0.6 16.4 %copy-start.2 = (bf16[2048,1,128]{2,0,1:T(8,128)(2,1)S(1)}, bf16[2048,1,128]{2,0,1:T(8,128)(2,1)}, u32[]{:S(2)}) copy-start(bf16[2048,1,128]{2,0,1:T(8,128)(2,1)} %param.9) | copy-start | bytes 1572868
  2.1 19.4 %copy-start.3 = (bf16[2048,1,128]{2,0,1:T(8,128)(2,1)S(1)}, bf16[2048,1,128]{2,0,1:T(8,128)(2,1)}, u32[]{:S(2)}) copy-start(bf16[2048,1,128]{2,0,1:T(8,128)(2,1)} %param.8) | copy-start | bytes 1572868
  3.2 30.8 %all-to-all-start = ((bf16[64,32,128]{2,1,0:T(8,128)(2,1)}), bf16[64,32,128]{2,1,0:T(8,128)(2,1)S(1)}, u32[]{:S(2)}, u32[]{:S(2)}) async-start(bf16[64,32,128]{2,1,0:T(8,128)(2,1)} %bitcast.44), calls=%async_computation | async-start | bytes 1048576 | tf_op jit(solution)/shard_map/all_to_all | solution.py:319
  17.0 11.9 %copy-start = (bf16[2048,1,128]{2,0,1:T(8,128)(2,1)S(1)}, bf16[2048,1,128]{2,0,1:T(8,128)(2,1)}, u32[]{:S(2)}) copy-start(bf16[2048,1,128]{2,0,1:T(8,128)(2,1)} %param.7) | copy-start | bytes 1572868
  17.8 26.7 %collective-permute-start.5 = (bf16[1024,128]{1,0:T(8,128)(2,1)}, bf16[1024,128]{1,0:T(8,128)(2,1)}, u32[]{:S(2)}, u32[]{:S(2)}) collective-permute-start(bf16[1024,128]{1,0:T(8,128)(2,1)} %broadcast_select_fusion.2), channel_id=1, source_target_pairs={{0,128},{192,64},{256,384},{448,320},{512,640},{704,576},{1,129},{... | collective-permute-start | bytes 786440 | tf_op jit(solution)/shard_map/ppermute | solution.py:308
  22.3 19.1 %collective-permute-start.1 = (bf16[1024,128]{1,0:T(8,128)(2,1)}, bf16[1024,128]{1,0:T(8,128)(2,1)S(1)}, u32[]{:S(2)}, u32[]{:S(2)}) collective-permute-start(bf16[1024,128]{1,0:T(8,128)(2,1)} %get-tuple-element.18), channel_id=1, source_target_pairs={{0,192},{64,0},{128,64},{192,128},{256,448},{320,256},{384,320},{4... | collective-permute-start | bytes 786440 | tf_op jit(solution)/shard_map/ppermute | solution.py:308
  24.3 18.8 %collective-permute-start = (bf16[1024,128]{1,0:T(8,128)(2,1)}, bf16[1024,128]{1,0:T(8,128)(2,1)S(1)}, u32[]{:S(2)}, u32[]{:S(2)}) collective-permute-start(bf16[1024,128]{1,0:T(8,128)(2,1)} %get-tuple-element.19), channel_id=1, source_target_pairs={{0,64},{64,128},{128,192},{192,0},{256,320},{320,384},{384,448},{4... | collective-permute-start | bytes 786440 | tf_op jit(solution)/shard_map/ppermute | solution.py:308
  34.1 2.4 %copy-start.1 = (bf16[64,32,128]{2,1,0:T(8,128)(2,1)}, bf16[64,32,128]{2,1,0:T(8,128)(2,1)S(1)}, u32[]{:S(2)}) copy-start(bf16[64,32,128]{2,1,0:T(8,128)(2,1)S(1)} %all-to-all-done) | copy-start | bytes 1572868
  34.2 74.2 %collective-permute-start.3 = (bf16[3072,128]{1,0:T(8,128)(2,1)S(1)}, bf16[3072,128]{1,0:T(8,128)(2,1)}, u32[]{:S(2)}, u32[]{:S(2)}) collective-permute-start(bf16[3072,128]{1,0:T(8,128)(2,1)S(1)} %pad_maximum_fusion), channel_id=1, source_target_pairs={{0,64},{64,128},{128,192},{256,320},{320,384},{384,448},{512,576},... | collective-permute-start | bytes 2359304 | tf_op jit(solution)/shard_map/ppermute | solution.py:308
  36.4 41.4 %copy-start.12 = (s32[192,4]{0,1:T(4,128)S(1)}, s32[192,4]{0,1:T(4,128)}, u32[]{:S(2)}) copy-start(s32[192,4]{0,1:T(4,128)} %param.12) | copy-start | bytes 9220
  36.4 71.9 %collective-permute-start.4 = (bf16[3072,128]{1,0:T(8,128)(2,1)}, bf16[3072,128]{1,0:T(8,128)(2,1)}, u32[]{:S(2)}, u32[]{:S(2)}) collective-permute-start(bf16[3072,128]{1,0:T(8,128)(2,1)} %pad_maximum_fusion.1), channel_id=1, source_target_pairs={{64,0},{128,64},{192,128},{320,256},{384,320},{448,384},{576,512},... | collective-permute-start | bytes 2359304 | tf_op jit(solution)/shard_map/ppermute | solution.py:308
  41.4 37.2 %copy-start.4 = (bf16[1024,128]{1,0:T(8,128)(2,1)}, bf16[1024,128]{1,0:T(8,128)(2,1)S(1)}, u32[]{:S(2)}) copy-start(bf16[1024,128]{1,0:T(8,128)(2,1)S(1)} %collective-permute-done.1.k_hi) | copy-start | bytes 786436
  41.5 21.1 %collective-permute-start.7 = (bf16[1024,128]{1,0:T(8,128)(2,1)S(1)}, bf16[1024,128]{1,0:T(8,128)(2,1)S(1)}, u32[]{:S(2)}, u32[]{:S(2)}) collective-permute-start(bf16[1024,128]{1,0:T(8,128)(2,1)S(1)} %broadcast_select_fusion.1), channel_id=1, source_target_pairs={{0,64},{192,128},{256,320},{448,384},{512,576},{704,640},{1,65},{1... | collective-permute-start | bytes 786440 | tf_op jit(solution)/shard_map/ppermute | solution.py:308
  43.1 35.6 %copy-start.5 = (bf16[1024,128]{1,0:T(8,128)(2,1)}, bf16[1024,128]{1,0:T(8,128)(2,1)S(1)}, u32[]{:S(2)}) copy-start(bf16[1024,128]{1,0:T(8,128)(2,1)S(1)} %collective-permute-done.k_lo) | copy-start | bytes 786436
  43.1 32.8 %collective-permute-start.2 = (bf16[1024,128]{1,0:T(8,128)(2,1)S(1)}, bf16[1024,128]{1,0:T(8,128)(2,1)S(1)}, u32[]{:S(2)}, u32[]{:S(2)}) collective-permute-start(bf16[1024,128]{1,0:T(8,128)(2,1)S(1)} %broadcast_select_fusion.3), channel_id=1, source_target_pairs={{0,256},{256,512},{448,192},{704,448},{1,257},{257,513},{449,193},... | collective-permute-start | bytes 786440 | tf_op jit(solution)/shard_map/ppermute | solution.py:308
  44.4 40.4 %collective-permute-start.6 = (bf16[1024,128]{1,0:T(8,128)(2,1)}, bf16[1024,128]{1,0:T(8,128)(2,1)S(1)}, u32[]{:S(2)}, u32[]{:S(2)}) collective-permute-start(bf16[1024,128]{1,0:T(8,128)(2,1)} %collective-permute-done.5), channel_id=1, source_target_pairs={{64,256},{320,512},{384,192},{640,448},{65,257},{321,513},{385,193... | collective-permute-start | bytes 786440 | tf_op jit(solution)/shard_map/ppermute | solution.py:308
  62.5 33.9 %collective-permute-start.8 = (bf16[1024,128]{1,0:T(8,128)(2,1)S(1)}, bf16[1024,128]{1,0:T(8,128)(2,1)S(1)}, u32[]{:S(2)}, u32[]{:S(2)}) collective-permute-start(bf16[1024,128]{1,0:T(8,128)(2,1)S(1)} %collective-permute-done.7), channel_id=1, source_target_pairs={{128,256},{320,192},{384,512},{576,448},{129,257},{321,193},{385,5... | collective-permute-start | bytes 786440 | tf_op jit(solution)/shard_map/ppermute | solution.py:308
  75.9 2.8 %copy-start.6 = (bf16[1024,128]{1,0:T(8,128)(2,1)}, bf16[1024,128]{1,0:T(8,128)(2,1)S(1)}, u32[]{:S(2)}) copy-start(bf16[1024,128]{1,0:T(8,128)(2,1)S(1)} %collective-permute-done.2.kz) | copy-start | bytes 786436
  75.9 32.4 %collective-permute-start.9 = (bf16[1024,128]{1,0:T(8,128)(2,1)S(1)}, bf16[1024,128]{1,0:T(8,128)(2,1)S(1)}, u32[]{:S(2)}, u32[]{:S(2)}) collective-permute-start(bf16[1024,128]{1,0:T(8,128)(2,1)S(1)} %broadcast_select_fusion), channel_id=1, source_target_pairs={{192,256},{256,192},{448,512},{512,448},{193,257},{257,193},{449,5... | collective-permute-start | bytes 786440 | tf_op jit(solution)/shard_map/ppermute | solution.py:308
  84.9 23.5 %copy-start.7 = (bf16[1024,128]{1,0:T(8,128)(2,1)}, bf16[1024,128]{1,0:T(8,128)(2,1)S(1)}, u32[]{:S(2)}) copy-start(bf16[1024,128]{1,0:T(8,128)(2,1)S(1)} %collective-permute-done.6.vz) | copy-start | bytes 786436
  84.9 13.5 %collective-permute-start.10 = (f32[16,128]{1,0:T(8,128)}, f32[16,128]{1,0:T(8,128)S(1)}, u32[]{:S(2)}, u32[]{:S(2)}) collective-permute-start(f32[16,128]{1,0:T(8,128)} %get-tuple-element.7), channel_id=1, source_target_pairs={{0,64},{64,128},{128,192},{192,256},{256,320},{320,384},{384,448},... | collective-permute-start | bytes 24584 | tf_op jit(solution)/shard_map/ppermute | solution.py:308
  96.5 11.9 %copy-start.8 = (bf16[1024,128]{1,0:T(8,128)(2,1)}, bf16[1024,128]{1,0:T(8,128)(2,1)S(1)}, u32[]{:S(2)}) copy-start(bf16[1024,128]{1,0:T(8,128)(2,1)S(1)} %collective-permute-done.8.qz) | copy-start | bytes 786436
  96.5 11.9 %collective-permute-start.11 = (f32[16,128]{1,0:T(8,128)}, f32[16,128]{1,0:T(8,128)S(1)}, u32[]{:S(2)}, u32[]{:S(2)}) collective-permute-start(f32[16,128]{1,0:T(8,128)} %get-tuple-element.8), channel_id=1, source_target_pairs={{64,0},{128,64},{192,128},{256,192},{320,256},{384,320},{448,384},... | collective-permute-start | bytes 24584 | tf_op jit(solution)/shard_map/ppermute | solution.py:308
  98.4 10.0 %copy-start.10 = (f32[16,128]{1,0:T(8,128)}, f32[16,128]{1,0:T(8,128)S(1)}, u32[]{:S(2)}) copy-start(f32[16,128]{1,0:T(8,128)S(1)} %collective-permute-done.10.slo) | copy-start | bytes 24580
  (2 other events, 1.3 us)
